TPU v7x, 256 devices: a whole 4x4x8 slice. The times are simulated.
256 devices in a mesh: ctx: 16 (over y, z_hi), head: 16 (over x, z_lo, core).
Axes of the slice: x: 4, y: 4, z: 8 (z_hi: 4, z_lo: 2; z = z_hi * 2 + z_lo), core: 2. Of those that a mesh axis runs over, the one named last changes fastest.
Arguments:
- queries: bfloat16 [16384, 4096], P('ctx', 'head'), parts along dimension 1, may hold values from -15 to 15
- key_rows: bfloat16 [16384, 2048], P('ctx', 'head'), parts along dimension 1, may hold values from -6 to 6
- value_rows: bfloat16 [16384, 2048], P('ctx', 'head'), parts along dimension 1, may hold values from -16 to 16
- block_order: int32 [16], replicated, may hold values from 0 to 15, each once
Outputs:
- attended: bfloat16 [16384, 4096], P('ctx', 'head'), parts along dimension 1
There are 16 independent parts, one for each index of `head`. A program takes and returns all parts, laid end to end along the dimension named above; an argument that names none is the same for every part. Nothing has to cross between parts.
Inputs may be any that keep to these rules, and one draw needn't show every extreme that they name: `block_order`: each block number appears once.
All inputs are finite; a program needn't handle non-finite values.
Results may differ from a plain program's by a relative error of at most 0.0033.
Values may be sent and summed in bfloat16 or wider, within the bound.
No kernel may reach another device: no remote copies, remote signals or barrier semaphores. Data moves between devices by JAX's collectives and lax.ppermute only.
A program may use at most 128 MiB of HBM per device.

v0:
```python
import jax
import jax.numpy as jnp
from jax import lax
from jax.experimental import pallas as pl
from jax.experimental.pallas import tpu as pltpu
from jax.sharding import PartitionSpec as P

HD = 128
QH = 2
TOK = 1024
ROWS = HD + 8
SCALE = 168.0 ** (-0.5) * 1.4426950408889634
VMEM = pl.BlockSpec(memory_space=pltpu.VMEM)
SMEM = pl.BlockSpec(memory_space=pltpu.SMEM)
ANY = pl.BlockSpec(memory_space=pl.ANY)
F32 = jnp.float32
BF16 = jnp.bfloat16


def dot_last(a, b):
    return lax.dot_general(a, b, (((1,), (1,)), ((), ())), preferred_element_type=F32)


def dot_mid(a, b):
    return lax.dot_general(a, b, (((1,), (0,)), ((), ())), preferred_element_type=F32)


def key_mate(y, core):
    return y ^ 1 if core == 0 else (((y - 1) % 4 ^ 1) + 1) % 4


def query_mate(y, core):
    return key_mate(y, 1 - core)


def mate_perm(mate):
    return [
        ((y * 4 + z) * 16 + h, (mate(y, h % 2) * 4 + z) * 16 + h)
        for y in range(4) for z in range(4) for h in range(16)
    ]


def ring_perm(sign):
    return [
        ((y * 4 + z) * 16 + h, (y * 4 + (z + (sign if h % 2 == 0 else -sign)) % 4) * 16 + h)
        for y in range(4) for z in range(4) for h in range(16)
    ]


def send(array, perm):
    return lax.ppermute(array, ("ctx", "head"), perm)


def head(ref, h):
    return ref[:, h * HD:(h + 1) * HD]


def absorb(kb, vt, q_ref, acc, shift):
    scores = [dot_last(kb[...], head(q_ref, 0)), None]
    for h in range(QH):
        if h + 1 < QH:
            scores[h + 1] = dot_last(kb[...], head(q_ref, h + 1))
        weights = jnp.exp2(scores[h] * SCALE - shift[h]).astype(BF16)
        acc[h] += dot_mid(vt[...], weights)


OWN, NEAR_A, NEAR_B, FAR = range(4)


def rank_of(meta, order, base, kind):
    index = meta[base]
    offset = (0, meta[3], 4 - meta[3], 2)[kind]
    return order[(index & 12) | ((index + offset) & 3)]


def diagonal_kernel(q_ref, kv_ref, acc, shift, vt):
    vt[HD:, :] = jnp.ones((8, TOK), BF16)
    vt[:HD, :] = kv_ref[:, HD:].T
    keys = lax.broadcasted_iota(jnp.int32, (TOK, TOK), 0)
    rows = lax.broadcasted_iota(jnp.int32, (TOK, TOK), 1)
    for h in range(QH):
        scores = dot_last(kv_ref[:, :HD], head(q_ref, h)) * SCALE
        scores = jnp.where(keys <= rows, scores, -jnp.inf)
        shift[h] = jnp.max(scores, axis=0, keepdims=True)
        weights = jnp.exp2(scores - shift[h]).astype(BF16)
        acc[h] = dot_mid(vt[...], weights)


def diagonal(q, kv):
    return pl.pallas_call(
        diagonal_kernel,
        out_shape=[
            jax.ShapeDtypeStruct((QH, ROWS, TOK), F32),
            jax.ShapeDtypeStruct((QH, 1, TOK), F32),
        ],
        in_specs=[VMEM, VMEM],
        out_specs=[VMEM, VMEM],
        scratch_shapes=[pltpu.VMEM((ROWS, TOK), BF16)],
        compiler_params=pltpu.CompilerParams(vmem_limit_bytes=32 << 20),
        cost_estimate=pl.CostEstimate(flops=3 << 30, bytes_accessed=4 << 20, transcendentals=2 << 20),
        name="diagonal",
    )(q, kv)


ACC = (QH, ROWS, TOK)
SHIFT = (QH, 1, TOK)
SCRATCH = [pltpu.VMEM((TOK, HD), BF16), pltpu.VMEM((ROWS, TOK), BF16), pltpu.SMEM((16,), jnp.int32)]


def run_units(meta, order, q_refs, q_ids, kv_refs, blocks, accs, shifts, kb, vt, flags):
    nq, nb = len(q_ids), len(blocks)
    vt[HD:, :] = jnp.ones((8, TOK), BF16)
    for n, block in enumerate(blocks):
        rank = rank_of(meta, order, *block)
        for q, q_id in enumerate(q_ids):
            flags[n * nq + q] = (rank < order[meta[q_id]]).astype(jnp.int32)

    def one(n):
        some = flags[n * nq]
        for q in range(1, nq):
            some += flags[n * nq + q]

        @pl.when(some > 0)
        def _():
            for place in range(nb):
                @pl.when(n == place)
                def _():
                    kb[...] = kv_refs[place][:, :HD]
                    vt[:HD, :] = kv_refs[place][:, HD:].T

            def query(q):
                @pl.when(flags[n * nq + q] > 0)
                def _():
                    absorb(kb, vt, q_refs.at[q], accs.at[q], shifts.at[q])

            if nq == 1:
                query(0)
            else:
                pl.loop(0, nq)(query)

    if nb == 1:
        one(0)
    else:
        pl.loop(0, nb)(one)


def stage(meta, order, qs, kvs, blocks, states):
    nk = len(kvs)
    first = states[0] is None
    old = list(states[1]) if first else list(states)

    def kernel(*refs):
        meta_ref, order_ref = refs[:2]
        q_refs = refs[2:4]
        kv_refs = refs[4:4 + nk]
        old_acc, old_shift, acc, shift, q_both, kb, vt, flags = refs[4 + nk:]
        for q in range(2):
            q_both[q] = q_refs[q][...]
        if first:
            acc[1] = old_acc[...]
            shift[1] = old_shift[...]
            acc[0] = jnp.zeros(ACC, F32)
            for h in range(QH):
                sample = dot_last(kv_refs[0][:HD, :HD], head(q_refs[0], h))
                shift[0, h] = jnp.max(sample, axis=0, keepdims=True) * SCALE
        else:
            acc[...] = old_acc[...]
            shift[...] = old_shift[...]
        run_units(meta_ref, order_ref, q_both, [2, 0], kv_refs, blocks, acc, shift, kb, vt, flags)

    return pl.pallas_call(
        kernel,
        out_shape=[jax.ShapeDtypeStruct((2,) + ACC, F32), jax.ShapeDtypeStruct((2,) + SHIFT, F32)],
        in_specs=[SMEM, SMEM] + [VMEM] * (4 + nk),
        out_specs=[VMEM, VMEM],
        scratch_shapes=[pltpu.VMEM((2, TOK, QH * HD), BF16)] + SCRATCH,
        compiler_params=pltpu.CompilerParams(vmem_limit_bytes=32 << 20),
        cost_estimate=pl.CostEstimate(
            flops=2 * len(blocks) << 31, bytes_accessed=8 << 20, transcendentals=2 * len(blocks) << 21
        ),
        name="stage",
    )(meta, order, *qs, *kvs, *old)


def recompute(meta, order, q_id, q_ref, sources, acc, shift, buf, kb, vt):
    query_rank = order[meta[q_id]]
    acc[0] = jnp.zeros(ACC, F32)
    shift[0] = jnp.full(SHIFT, -1e30, F32)

    for n, source in enumerate(sources):
        rank = rank_of(meta, order, n // 4, n % 4)

        @pl.when(rank <= query_rank)
        def _():
            pltpu.sync_copy(source, buf)
            kb[...] = buf[:, :HD]
            vt[:HD, :] = buf[:, HD:].T

            @pl.loop(0, 16)
            def _(tile):
                h, start = tile & 1, pl.multiple_of((tile >> 1) * HD, HD)
                cols = pl.ds(start, HD)
                keys = lax.broadcasted_iota(jnp.int32, (TOK, HD), 0) + rank * TOK
                rows = lax.broadcasted_iota(jnp.int32, (TOK, HD), 1) + query_rank * TOK + start
                query = q_ref[cols, pl.ds(pl.multiple_of(h * HD, HD), HD)]
                scores = dot_last(kb[...], query) * SCALE
                scores = jnp.where(keys <= rows, scores, -jnp.inf)
                old = shift[0, h, :, cols]
                new = jnp.maximum(old, jnp.max(scores, axis=0, keepdims=True))
                weights = jnp.exp2(scores - new).astype(BF16)
                acc[0, h, :, cols] = acc[0, h, :, cols] * jnp.exp2(old - new) + dot_mid(vt[...], weights)
                shift[0, h, :, cols] = new


def closing(meta, order, q, q_id, kvs, blocks, state, everything, pack):
    nk, ne = len(kvs), len(everything)
    place = 0 if q_id == 2 else 1

    def kernel(*refs):
        meta_ref, order_ref, q_ref = refs[:3]
        kv_refs = refs[3:3 + nk]
        old_acc, old_shift = refs[3 + nk:5 + nk]
        all_refs = refs[5 + nk:5 + nk + ne]
        rest = refs[5 + nk + ne:]
        if pack:
            sent, acc, shift, buf, q_one, kb, vt, flags = rest
        else:
            acc, shift, buf, q_one, kb, vt, flags = rest
        at = place if old_acc.shape[0] == 2 else 0
        acc[0] = old_acc[at]
        shift[0] = old_shift[at]
        q_one[0] = q_ref[...]
        run_units(meta_ref, order_ref, q_one, [q_id], kv_refs, blocks, acc, shift, kb, vt, flags)
        if not ne:
            return
        query_rank = order_ref[meta_ref[q_id]]
        active = jnp.int32(0)
        for n in range(8):
            active += (rank_of(meta_ref, order_ref, n // 4, n % 4) <= query_rank).astype(jnp.int32)
        totals = jnp.concatenate([acc[0, h, HD:HD + 1, :] for h in range(QH)], axis=0)
        fine = jnp.logical_and(totals > 2.0 ** -60, totals < 2.0 ** 100)
        faults = jnp.sum(jnp.where(fine, 0.0, 1.0))

        @pl.when(jnp.logical_and(active > 0, faults > 0.0))
        def _():
            recompute(meta_ref, order_ref, q_id, q_ref, all_refs, acc, shift, buf, kb, vt)

        if pack:
            for h in range(QH):
                total = acc[0, h, HD:HD + 1, :]
                empty = total <= 0.0
                safe = jnp.where(empty, 1.0, total)
                sent[h * HD:(h + 1) * HD, :] = (acc[0, h, :HD, :] * (1.0 / safe)).astype(BF16)
                level = jnp.where(empty, -1e30, shift[0, h] + jnp.log2(safe))
                first = level.astype(BF16).astype(F32)
                second = (level - first).astype(BF16).astype(F32)
                third = level - first - second
                row = lax.broadcasted_iota(jnp.int32, (8, TOK), 0)
                packed = jnp.where(row == 0, first, jnp.where(row == 1, second, third))
                sent[QH * HD + 8 * h:QH * HD + 8 * h + 8, :] = packed.astype(BF16)

    state_shapes = [((1,) + ACC, F32), ((1,) + SHIFT, F32)]
    scratch = [pltpu.VMEM((TOK, 2 * HD), BF16), pltpu.VMEM((1, TOK, QH * HD), BF16)] + SCRATCH
    if pack:
        out_shape = jax.ShapeDtypeStruct((QH * HD + 16, TOK), BF16)
        out_specs = VMEM
        scratch = [pltpu.VMEM(*s) for s in state_shapes] + scratch
    else:
        out_shape = [jax.ShapeDtypeStruct(*s) for s in state_shapes]
        out_specs = [VMEM, VMEM]
    return pl.pallas_call(
        kernel,
        out_shape=out_shape,
        in_specs=[SMEM, SMEM] + [VMEM] * (3 + nk) + [ANY] * ne,
        out_specs=out_specs,
        scratch_shapes=scratch,
        compiler_params=pltpu.CompilerParams(vmem_limit_bytes=32 << 20),
        cost_estimate=pl.CostEstimate(
            flops=len(blocks) << 31, bytes_accessed=8 << 20, transcendentals=len(blocks) << 21
        ),
        name="away" if pack else "home" if ne else "guest",
    )(meta, order, q, *kvs, *state, *everything)


def join_kernel(acc, shift, came, out):
    for h in range(QH):
        total = acc[0, h, HD:HD + 1, :]
        here = shift[0, h] + jnp.log2(total)
        at = QH * HD + 8 * h
        level = came[at:at + 8, :].astype(F32)
        there = level[0:1] + level[1:2] + level[2:3]
        top = jnp.maximum(here, there)
        own, far = jnp.exp2(here - top), jnp.exp2(there - top)
        both = own + far
        mixed = acc[0, h, :HD, :] * (own / (total * both)) + came[h * HD:(h + 1) * HD, :].astype(F32) * (far / both)
        out[:, h * HD:(h + 1) * HD] = mixed.T.astype(BF16)


def join(state, came):
    return pl.pallas_call(
        join_kernel,
        out_shape=jax.ShapeDtypeStruct((TOK, QH * HD), BF16),
        in_specs=[VMEM] * 3,
        out_specs=VMEM,
        compiler_params=pltpu.CompilerParams(vmem_limit_bytes=32 << 20),
        name="join",
    )(*state, came)


def after(array, *others):
    return lax.optimization_barrier((array,) + others)[0]


def body(q0, keys, values, order):
    index = lax.axis_index("ctx")
    core = lax.axis_index("head") & 1
    y, z = index >> 2, index & 3
    even, odd = y ^ 1, (((y + 3) & 3 ^ 1) + 1) & 3
    key_y = jnp.where(core == 0, even, odd)
    query_y = jnp.where(core == 0, odd, even)
    meta = jnp.stack([index, key_y * 4 + z, query_y * 4 + z, jnp.where(core == 0, 3, 1)]).astype(jnp.int32)

    key_perm, query_perm = mate_perm(key_mate), mate_perm(query_mate)
    forth, back = ring_perm(1), ring_perm(-1)
    kv = jnp.concatenate([keys, values], axis=1)
    near_a = send(kv, forth)
    mate_own = send(kv, key_perm)
    q1 = send(q0, query_perm)
    state0 = diagonal(q0, kv)

    near_b = send(after(kv, near_a), back)
    mate_a = send(near_a, key_perm)
    qs = [after(q1, near_a), q0]
    state = stage(meta, order, qs, [kv, mate_own], [(0, OWN), (1, OWN)], [None, state0])

    far = send(after(near_a, near_b), forth)
    near_b = after(near_b, state[1])
    mate_b = send(near_b, key_perm)
    state = stage(
        meta, order, qs, [near_a, after(mate_a, near_b)], [(0, NEAR_A), (1, NEAR_A)], state
    )

    far = after(far, state[1])
    mate_far = send(far, key_perm)
    guest = closing(
        meta, order, q1, 2, [near_b, after(mate_b, far), far], [(0, NEAR_B), (1, NEAR_B), (0, FAR)], state, [], False
    )
    everything = [kv, near_a, near_b, far, mate_own, mate_a, mate_b, mate_far]
    away = closing(meta, order, q1, 2, [mate_far], [(1, FAR)], guest, everything, True)
    came = send(away, query_perm)
    own = closing(
        meta, order, q0, 0, [near_b, mate_b, far, mate_far],
        [(0, NEAR_B), (1, NEAR_B), (0, FAR), (1, FAR)], state, everything, False,
    )
    return join(own, came)


def solution(mesh):
    in_specs = (P("ctx", "head"), P("ctx", "head"), P("ctx", "head"), P())
    return jax.shard_map(body, mesh=mesh, in_specs=in_specs, out_specs=P("ctx", "head"), check_vma=False)
```

profile of v0, /device:TPU:6, one launch (start us, length us, event | category | flops | bytes accessed | tf_op | source)
XLA Modules:
  0.0 77.3 jit_solution(12125200352849056737)
XLA Ops:
  0.0 1.0 %constant_dynamic-update-slice_fusion.1 = bf16[1024,256]{1,0:T(8,128)(2,1)S(1)} fusion(bf16[1024,128]{1,0:T(8,128)(2,1)} %param.5), kind=kLoop, calls=%fused_computation.1 | loop fusion | bytes 524288
  1.0 1.0 %constant_dynamic-update-slice_fusion.kv_ref.refs_4_.refs_9_.refs_6_ = bf16[1024,256]{1,0:T(8,128)(2,1)S(1)} fusion(bf16[1024,256]{1,0:T(8,128)(2,1)S(1)} %constant_dynamic-update-slice_fusion.1, bf16[1024,128]{1,0:T(8,128)(2,1)} %param.6), kind=kLoop, calls=%fused_computation | loop fusion | bytes 524288 | tf_op jit(solution)/shard_map/concatenate | solution.py:325
  2.0 3.3 %collective-permute-start = (bf16[1024,256]{1,0:T(8,128)(2,1)S(1)}, bf16[1024,256]{1,0:T(8,128)(2,1)S(1)}, u32[]{:S(2)}, u32[]{:S(2)}) collective-permute-start(bf16[1024,256]{1,0:T(8,128)(2,1)S(1)} %constant_dynamic-update-slice_fusion.kv_ref.refs_4_.refs_9_.refs_6_), channel_id=1, source_target_pairs={{0,16},{1,49},{2,18},{3,51},{4,20},{5,53},{6,22},{7,55},{8,24},{9,... | collective-permute-start | bytes 1572872 | tf_op jit(solution)/shard_map/ppermute | solution.py:51
  5.4 3.0 %collective-permute-start.2 = (bf16[1024,256]{1,0:T(8,128)(2,1)}, bf16[1024,256]{1,0:T(8,128)(2,1)S(1)}, u32[]{:S(2)}, u32[]{:S(2)}) collective-permute-start(bf16[1024,256]{1,0:T(8,128)(2,1)} %refs_2_.1), channel_id=1, source_target_pairs={{0,192},{1,65},{2,194},{3,67},{4,196},{5,69},{6,198},{7,71},{8,200... | collective-permute-start | bytes 1572872 | tf_op jit(solution)/shard_map/ppermute | solution.py:51
  8.4 0.1 collective-permute-start.3
  8.6 1.0 %copy-done = bf16[1024,256]{1,0:T(8,128)(2,1)S(1)} copy-done((bf16[1024,256]{1,0:T(8,128)(2,1)S(1)}, bf16[1024,256]{1,0:T(8,128)(2,1)}, u32[]{:S(2)}) %copy-start) | copy-done | bytes 524312
  9.6 2.5 %diagonal.1 = (f32[2,136,1024]{2,1,0:T(8,128)S(1)}, f32[2,1,1024]{2,1,0:T(1,128)S(1)}) custom-call(bf16[1024,256]{1,0:T(8,128)(2,1)S(1)} %copy-done, bf16[1024,256]{1,0:T(8,128)(2,1)S(1)} %constant_dynamic-update-slice_fusion.kv_ref.refs_4_.refs_9_.refs_6_), custom_call_target="tpu_custom_call" | custom-call | flops 3221225472 | bytes 4194304 | tf_op jit(solution)/shard_map/diagonal/pallas_call | solution.py:90
  12.1 5.4 %collective-permute-done.refs_4_.refs_10_.refs_7_ = bf16[1024,256]{1,0:T(8,128)(2,1)S(1)} collective-permute-done((bf16[1024,256]{1,0:T(8,128)(2,1)S(1)}, bf16[1024,256]{1,0:T(8,128)(2,1)S(1)}, u32[]{:S(2)}, u32[]{:S(2)}) %collective-permute-start) | collective-permute-done | bytes 524320 | tf_op jit(solution)/shard_map/ppermute | solution.py:51
  17.5 1.6 %collective-permute-done.2.refs_2_ = bf16[1024,256]{1,0:T(8,128)(2,1)S(1)} collective-permute-done((bf16[1024,256]{1,0:T(8,128)(2,1)}, bf16[1024,256]{1,0:T(8,128)(2,1)S(1)}, u32[]{:S(2)}, u32[]{:S(2)}) %collective-permute-start.2) | collective-permute-done | bytes 524320 | tf_op jit(solution)/shard_map/ppermute | solution.py:51
  19.1 5.1 %collective-permute-start.1 = (bf16[1024,256]{1,0:T(8,128)(2,1)S(1)}, bf16[1024,256]{1,0:T(8,128)(2,1)S(1)}, u32[]{:S(2)}, u32[]{:S(2)}) collective-permute-start(bf16[1024,256]{1,0:T(8,128)(2,1)S(1)} %constant_dynamic-update-slice_fusion.kv_ref.refs_4_.refs_9_.refs_6_), channel_id=1, source_target_pairs={{0,48},{1,17},{2,50},{3,19},{4,52},{5,21},{6,54},{7,23},{8,56},{9,... | collective-permute-start | bytes 1572872 | tf_op jit(solution)/shard_map/ppermute | solution.py:51
  24.1 1.6 %collective-permute-start.6 = (bf16[1024,256]{1,0:T(8,128)(2,1)S(1)}, bf16[1024,256]{1,0:T(8,128)(2,1)S(1)}, u32[]{:S(2)}, u32[]{:S(2)}) collective-permute-start(bf16[1024,256]{1,0:T(8,128)(2,1)S(1)} %collective-permute-done.refs_4_.refs_10_.refs_7_), channel_id=1, source_target_pairs={{0,64},{1,193},{2,66},{3,195},{4,68},{5,197},{6,70},{7,199},{8,72}... | collective-permute-start | bytes 1572872 | tf_op jit(solution)/shard_map/ppermute | solution.py:51
  25.7 5.2 %stage.2 = (f32[2,2,136,1024]{3,2,1,0:T(8,128)S(1)}, f32[2,2,1,1024]{3,2,1,0:T(1,128)S(1)}) custom-call(s32[4]{0:T(128)S(1)} %pad_add_fusion.refs_0_, s32[16]{0:T(128)S(1)} %copy-done.2, bf16[1024,256]{1,0:T(8,128)(2,1)S(1)} %collective-permute-done.2.refs_2_, bf16[1024,256]{1,0:T(8,128)(2,1)S(1)} %copy-done, ...), custom_call_target="tpu_custom_call" | custom-call | flops 8589934592 | bytes 8388608 | tf_op jit(solution)/shard_map/stage/pallas_call | solution.py:171
  30.9 5.5 %collective-permute-done.1.refs_3_.refs_11_.refs_8_ = bf16[1024,256]{1,0:T(8,128)(2,1)S(1)} collective-permute-done((bf16[1024,256]{1,0:T(8,128)(2,1)S(1)}, bf16[1024,256]{1,0:T(8,128)(2,1)S(1)}, u32[]{:S(2)}, u32[]{:S(2)}) %collective-permute-start.1) | collective-permute-done | bytes 524320 | tf_op jit(solution)/shard_map/ppermute | solution.py:51
  36.5 1.6 %collective-permute-start.4 = (bf16[1024,256]{1,0:T(8,128)(2,1)S(1)}, bf16[1024,256]{1,0:T(8,128)(2,1)S(1)}, u32[]{:S(2)}, u32[]{:S(2)}) collective-permute-start(bf16[1024,256]{1,0:T(8,128)(2,1)S(1)} %collective-permute-done.1.refs_3_.refs_11_.refs_8_), channel_id=1, source_target_pairs={{0,64},{1,193},{2,66},{3,195},{4,68},{5,197},{6,70},{7,199},{8,72}... | collective-permute-start | bytes 1572872 | tf_op jit(solution)/shard_map/ppermute | solution.py:51
  38.0 2.5 %collective-permute-start.5 = (bf16[1024,256]{1,0:T(8,128)(2,1)S(1)}, bf16[1024,256]{1,0:T(8,128)(2,1)S(1)}, u32[]{:S(2)}, u32[]{:S(2)}) collective-permute-start(bf16[1024,256]{1,0:T(8,128)(2,1)S(1)} %collective-permute-done.refs_4_.refs_10_.refs_7_), channel_id=1, source_target_pairs={{0,16},{1,49},{2,18},{3,51},{4,20},{5,53},{6,22},{7,55},{8,24},{9,... | collective-permute-start | bytes 1572872 | tf_op jit(solution)/shard_map/ppermute | solution.py:51
  40.5 2.9 %stage.3 = (f32[2,2,136,1024]{3,2,1,0:T(8,128)S(1)}, f32[2,2,1,1024]{3,2,1,0:T(1,128)S(1)}) custom-call(s32[4]{0:T(128)S(1)} %pad_add_fusion.refs_0_, s32[16]{0:T(128)S(1)} %copy-done.2, bf16[1024,256]{1,0:T(8,128)(2,1)S(1)} %collective-permute-done.2.refs_2_, bf16[1024,256]{1,0:T(8,128)(2,1)S(1)} %copy-done, ...), custom_call_target="tpu_custom_call" | custom-call | flops 8589934592 | bytes 8388608 | tf_op jit(solution)/shard_map/stage/pallas_call | solution.py:171
  43.4 9.5 %collective-permute-done.5.refs_5_.refs_12_.refs_9_ = bf16[1024,256]{1,0:T(8,128)(2,1)S(1)} collective-permute-done((bf16[1024,256]{1,0:T(8,128)(2,1)S(1)}, bf16[1024,256]{1,0:T(8,128)(2,1)S(1)}, u32[]{:S(2)}, u32[]{:S(2)}) %collective-permute-start.5) | collective-permute-done | bytes 524320 | tf_op jit(solution)/shard_map/ppermute | solution.py:51
  52.8 2.0 %collective-permute-start.7 = (bf16[1024,256]{1,0:T(8,128)(2,1)S(1)}, bf16[1024,256]{1,0:T(8,128)(2,1)S(1)}, u32[]{:S(2)}, u32[]{:S(2)}) collective-permute-start(bf16[1024,256]{1,0:T(8,128)(2,1)S(1)} %collective-permute-done.5.refs_5_.refs_12_.refs_9_), channel_id=1, source_target_pairs={{0,64},{1,193},{2,66},{3,195},{4,68},{5,197},{6,70},{7,199},{8,72}... | collective-permute-start | bytes 1572872 | tf_op jit(solution)/shard_map/ppermute | solution.py:51
  54.8 6.7 %guest.1 = (f32[1,2,136,1024]{3,2,1,0:T(8,128)S(1)}, f32[1,2,1,1024]{3,2,1,0:T(1,128)S(1)}) custom-call(s32[4]{0:T(128)S(1)} %pad_add_fusion.refs_0_, s32[16]{0:T(128)S(1)} %copy-done.2, bf16[1024,256]{1,0:T(8,128)(2,1)S(1)} %collective-permute-done.2.refs_2_, bf16[1024,256]{1,0:T(8,128)(2,1)S(1)} %collective-permute-done.1.refs_3_.refs_11_.refs_8_, ...), custom_call_target="tpu_custom_call" | custom-call | flops 6442450944 | bytes 8388608 | tf_op jit(solution)/shard_map/guest/pallas_call | solution.py:271
  61.6 0.4 collective-permute-done.7.refs_6_.refs_16_.refs_3_.refs_13_
  62.0 2.9 %away.1 = bf16[272,1024]{1,0:T(8,128)(2,1)S(1)} custom-call(s32[4]{0:T(128)S(1)} %pad_add_fusion.refs_0_, s32[16]{0:T(128)S(1)} %copy-done.2, bf16[1024,256]{1,0:T(8,128)(2,1)S(1)} %collective-permute-done.2.refs_2_, bf16[1024,256]{1,0:T(8,128)(2,1)S(1)} %collective-permute-done.7.refs_6_.refs_16_.refs_3_.refs_13_, ...), custom_call_target="tpu_custom_call" | custom-call | flops 2147483648 | bytes 8388608 | tf_op jit(solution)/shard_map/away/pallas_call | solution.py:271
  65.0 2.1 %collective-permute-start.8 = (bf16[272,1024]{1,0:T(8,128)(2,1)S(1)}, bf16[272,1024]{1,0:T(8,128)(2,1)S(1)}, u32[]{:S(2)}, u32[]{:S(2)}) collective-permute-start(bf16[272,1024]{1,0:T(8,128)(2,1)S(1)} %away.1), channel_id=1, source_target_pairs={{0,192},{1,65},{2,194},{3,67},{4,196},{5,69},{6,198},{7,71},{8,200... | collective-permute-start | bytes 1671176 | tf_op jit(solution)/shard_map/ppermute | solution.py:51
  67.1 9.1 %home.1 = (f32[1,2,136,1024]{3,2,1,0:T(8,128)S(1)}, f32[1,2,1,1024]{3,2,1,0:T(1,128)S(1)}) custom-call(s32[4]{0:T(128)S(1)} %pad_add_fusion.refs_0_, s32[16]{0:T(128)S(1)} %copy-done.2, bf16[1024,256]{1,0:T(8,128)(2,1)S(1)} %copy-done.1, bf16[1024,256]{1,0:T(8,128)(2,1)S(1)} %collective-permute-done.1.refs_3_.refs_11_.refs_8_, ...), custom_call_target="tpu_custom_call" | custom-call | flops 8589934592 | bytes 8388608 | tf_op jit(solution)/shard_map/home/pallas_call | solution.py:271
  76.2 1.1 %join.1 = bf16[1024,256]{1,0:T(8,128)(2,1)} custom-call(f32[1,2,136,1024]{3,2,1,0:T(8,128)S(1)} %get-tuple-element.34.acc, f32[1,2,1,1024]{3,2,1,0:T(1,128)S(1)} %get-tuple-element.35.shift, bf16[272,1024]{1,0:T(8,128)(2,1)S(1)} %collective-permute-done.8.came), custom_call_target="tpu_custom_call" | custom-call | tf_op jit(solution)/shard_map/join/pallas_call | solution.py:300
  (10 shorter events, 0.1 us)
Async XLA Ops:
  2.0 15.5 %collective-permute-start = (bf16[1024,256]{1,0:T(8,128)(2,1)S(1)}, bf16[1024,256]{1,0:T(8,128)(2,1)S(1)}, u32[]{:S(2)}, u32[]{:S(2)}) collective-permute-start(bf16[1024,256]{1,0:T(8,128)(2,1)S(1)} %constant_dynamic-update-slice_fusion.kv_ref.refs_4_.refs_9_.refs_6_), channel_id=1, source_target_pairs={{0,16},{1,49},{2,18},{3,51},{4,20},{5,53},{6,22},{7,55},{8,24},{9,... | collective-permute-start | bytes 1572872 | tf_op jit(solution)/shard_map/ppermute | solution.py:51
  5.4 13.7 %collective-permute-start.2 = (bf16[1024,256]{1,0:T(8,128)(2,1)}, bf16[1024,256]{1,0:T(8,128)(2,1)S(1)}, u32[]{:S(2)}, u32[]{:S(2)}) collective-permute-start(bf16[1024,256]{1,0:T(8,128)(2,1)} %refs_2_.1), channel_id=1, source_target_pairs={{0,192},{1,65},{2,194},{3,67},{4,196},{5,69},{6,198},{7,71},{8,200... | collective-permute-start | bytes 1572872 | tf_op jit(solution)/shard_map/ppermute | solution.py:51
  8.4 17.3 %collective-permute-start.3 = (bf16[1024,256]{1,0:T(8,128)(2,1)S(1)}, bf16[1024,256]{1,0:T(8,128)(2,1)S(1)}, u32[]{:S(2)}, u32[]{:S(2)}) collective-permute-start(bf16[1024,256]{1,0:T(8,128)(2,1)S(1)} %constant_dynamic-update-slice_fusion.kv_ref.refs_4_.refs_9_.refs_6_), channel_id=1, source_target_pairs={{0,64},{1,193},{2,66},{3,195},{4,68},{5,197},{6,70},{7,199},{8,72}... | collective-permute-start | bytes 1572872 | tf_op jit(solution)/shard_map/ppermute | solution.py:51
  8.6 1.0 %copy-start = (bf16[1024,256]{1,0:T(8,128)(2,1)S(1)}, bf16[1024,256]{1,0:T(8,128)(2,1)}, u32[]{:S(2)}) copy-start(bf16[1024,256]{1,0:T(8,128)(2,1)} %refs_2_.1) | copy-start | bytes 1572868
  9.6 16.1 %copy-start.2 = (s32[16]{0:T(128)S(1)}, s32[16]{0:T(128)}, u32[]{:S(2)}) copy-start(s32[16]{0:T(128)} %refs_1_.9) | copy-start | bytes 196
  19.1 17.4 %collective-permute-start.1 = (bf16[1024,256]{1,0:T(8,128)(2,1)S(1)}, bf16[1024,256]{1,0:T(8,128)(2,1)S(1)}, u32[]{:S(2)}, u32[]{:S(2)}) collective-permute-start(bf16[1024,256]{1,0:T(8,128)(2,1)S(1)} %constant_dynamic-update-slice_fusion.kv_ref.refs_4_.refs_9_.refs_6_), channel_id=1, source_target_pairs={{0,48},{1,17},{2,50},{3,19},{4,52},{5,21},{6,54},{7,23},{8,56},{9,... | collective-permute-start | bytes 1572872 | tf_op jit(solution)/shard_map/ppermute | solution.py:51
  24.1 13.9 %collective-permute-start.6 = (bf16[1024,256]{1,0:T(8,128)(2,1)S(1)}, bf16[1024,256]{1,0:T(8,128)(2,1)S(1)}, u32[]{:S(2)}, u32[]{:S(2)}) collective-permute-start(bf16[1024,256]{1,0:T(8,128)(2,1)S(1)} %collective-permute-done.refs_4_.refs_10_.refs_7_), channel_id=1, source_target_pairs={{0,64},{1,193},{2,66},{3,195},{4,68},{5,197},{6,70},{7,199},{8,72}... | collective-permute-start | bytes 1572872 | tf_op jit(solution)/shard_map/ppermute | solution.py:51
  36.5 18.4 %collective-permute-start.4 = (bf16[1024,256]{1,0:T(8,128)(2,1)S(1)}, bf16[1024,256]{1,0:T(8,128)(2,1)S(1)}, u32[]{:S(2)}, u32[]{:S(2)}) collective-permute-start(bf16[1024,256]{1,0:T(8,128)(2,1)S(1)} %collective-permute-done.1.refs_3_.refs_11_.refs_8_), channel_id=1, source_target_pairs={{0,64},{1,193},{2,66},{3,195},{4,68},{5,197},{6,70},{7,199},{8,72}... | collective-permute-start | bytes 1572872 | tf_op jit(solution)/shard_map/ppermute | solution.py:51
  38.0 14.8 %collective-permute-start.5 = (bf16[1024,256]{1,0:T(8,128)(2,1)S(1)}, bf16[1024,256]{1,0:T(8,128)(2,1)S(1)}, u32[]{:S(2)}, u32[]{:S(2)}) collective-permute-start(bf16[1024,256]{1,0:T(8,128)(2,1)S(1)} %collective-permute-done.refs_4_.refs_10_.refs_7_), channel_id=1, source_target_pairs={{0,16},{1,49},{2,18},{3,51},{4,20},{5,53},{6,22},{7,55},{8,24},{9,... | collective-permute-start | bytes 1572872 | tf_op jit(solution)/shard_map/ppermute | solution.py:51
  52.8 9.2 %collective-permute-start.7 = (bf16[1024,256]{1,0:T(8,128)(2,1)S(1)}, bf16[1024,256]{1,0:T(8,128)(2,1)S(1)}, u32[]{:S(2)}, u32[]{:S(2)}) collective-permute-start(bf16[1024,256]{1,0:T(8,128)(2,1)S(1)} %collective-permute-done.5.refs_5_.refs_12_.refs_9_), channel_id=1, source_target_pairs={{0,64},{1,193},{2,66},{3,195},{4,68},{5,197},{6,70},{7,199},{8,72}... | collective-permute-start | bytes 1572872 | tf_op jit(solution)/shard_map/ppermute | solution.py:51
  62.0 5.0 %copy-start.1 = (bf16[1024,256]{1,0:T(8,128)(2,1)S(1)}, bf16[1024,256]{1,0:T(8,128)(2,1)}, u32[]{:S(2)}) copy-start(bf16[1024,256]{1,0:T(8,128)(2,1)} %refs_2_.1) | copy-start | bytes 1572868
  65.0 11.2 %collective-permute-start.8 = (bf16[272,1024]{1,0:T(8,128)(2,1)S(1)}, bf16[272,1024]{1,0:T(8,128)(2,1)S(1)}, u32[]{:S(2)}, u32[]{:S(2)}) collective-permute-start(bf16[272,1024]{1,0:T(8,128)(2,1)S(1)} %away.1), channel_id=1, source_target_pairs={{0,192},{1,65},{2,194},{3,67},{4,196},{5,69},{6,198},{7,71},{8,200... | collective-permute-start | bytes 1671176 | tf_op jit(solution)/shard_map/ppermute | solution.py:51
where the time goes:
time: 77.4 us; the launch traced here: 77.3 us
  Pallas kernels  30.5 us (39%)
  waiting for transfers between devices  22.4 us (29%)
  starting transfers between devices  21.2 us (27%)
  local copies, waits for them, and re-layouts  3.06 us (4%)
    ppermute x9, waiting for transfers between devices, send(): return lax.ppermute(array, ('ctx', 'head'), perm)  22.4 us
    ppermute x9, starting transfers between devices, send(): return lax.ppermute(array, ('ctx', 'head'), perm)  21.2 us
    pallas_call x3, Pallas kernels, closing(): pl.pallas_call(kernel, out_shape=out_shape, in_specs=[SMEM, SMEM] + [VMEM...  18.8 us
    pallas_call x2, Pallas kernels, stage(): pl.pallas_call(kernel, out_shape=[jax.ShapeDtypeStruct((2,) + ACC, F32),...  8.07 us
    pallas_call x1, Pallas kernels, diagonal(): pl.pallas_call(diagonal_kernel, out_shape=[jax.ShapeDtypeStruct((QH, ROWS...  2.49 us
    unnamed x7, local copies, waits for them, and re-layouts  2.04 us
  transfers between devices with their start and end apart: 9, of which 5 were waited for; matrix products, arithmetic and copies ran while one was open for 0% of the time, Pallas kernels for 34%

commit v1 on v0

--- a/solution.py
+++ b/solution.py
@@ -311,6 +311,21 @@
     return lax.optimization_barrier((array,) + others)[0]
 
 
+def pack_kernel(keys, values, kv):
+    kv[:, :HD] = keys[...]
+    kv[:, HD:] = values[...]
+
+
+def packed_kv(keys, values):
+    return pl.pallas_call(
+        pack_kernel,
+        out_shape=jax.ShapeDtypeStruct((TOK, 2 * HD), BF16),
+        in_specs=[VMEM] * 2,
+        out_specs=VMEM,
+        name="pack_kv",
+    )(keys, values)
+
+
 def body(q0, keys, values, order):
     index = lax.axis_index("ctx")
     core = lax.axis_index("head") & 1
@@ -322,35 +337,32 @@
 
     key_perm, query_perm = mate_perm(key_mate), mate_perm(query_mate)
     forth, back = ring_perm(1), ring_perm(-1)
-    kv = jnp.concatenate([keys, values], axis=1)
+    kv = packed_kv(keys, values)
     near_a = send(kv, forth)
+    near_b = send(kv, back)
     mate_own = send(kv, key_perm)
     q1 = send(q0, query_perm)
     state0 = diagonal(q0, kv)
-
-    near_b = send(after(kv, near_a), back)
+    qs = [q1, q0]
+    state = stage(meta, order, qs, [kv, mate_own], [(0, OWN), (1, OWN)], [None, state0])
+
+    near_a, near_b = after((near_a, near_b), state[1])
+    far = send(near_a, forth)
     mate_a = send(near_a, key_perm)
-    qs = [after(q1, near_a), q0]
-    state = stage(meta, order, qs, [kv, mate_own], [(0, OWN), (1, OWN)], [None, state0])
-
-    far = send(after(near_a, near_b), forth)
-    near_b = after(near_b, state[1])
     mate_b = send(near_b, key_perm)
-    state = stage(
-        meta, order, qs, [near_a, after(mate_a, near_b)], [(0, NEAR_A), (1, NEAR_A)], state
-    )
-
-    far = after(far, state[1])
+    state = stage(meta, order, [q1, after(q0, near_a, near_b)], [near_a, near_b], [(0, NEAR_A), (0, NEAR_B)], state)
+
+    far, mate_a, mate_b = after((far, mate_a, mate_b), state[1])
     mate_far = send(far, key_perm)
     guest = closing(
-        meta, order, q1, 2, [near_b, after(mate_b, far), far], [(0, NEAR_B), (1, NEAR_B), (0, FAR)], state, [], False
+        meta, order, q1, 2, [after(mate_a, far), mate_b, far], [(1, NEAR_A), (1, NEAR_B), (0, FAR)], state, [], False
     )
     everything = [kv, near_a, near_b, far, mate_own, mate_a, mate_b, mate_far]
     away = closing(meta, order, q1, 2, [mate_far], [(1, FAR)], guest, everything, True)
     came = send(away, query_perm)
     own = closing(
-        meta, order, q0, 0, [near_b, mate_b, far, mate_far],
-        [(0, NEAR_B), (1, NEAR_B), (0, FAR), (1, FAR)], state, everything, False,
+        meta, order, q0, 0, [mate_a, mate_b, far, mate_far],
+        [(1, NEAR_A), (1, NEAR_B), (0, FAR), (1, FAR)], state, everything, False,
     )
     return join(own, came)
 

time: 77.4 us -> 74.7 us (0.965)
  the two profiles are of different devices: /device:TPU:6 before, /device:TPU:68 now
where the time goes in v1:
time: 74.7 us; the launch traced here: 75.1 us
  Pallas kernels  33.8 us (45%)
  waiting for transfers between devices  22.6 us (30%)
  starting transfers between devices  16.4 us (22%)
  local copies, waits for them, and re-layouts  2.12 us (3%)
    ppermute x9, waiting for transfers between devices, send(): return lax.ppermute(array, ('ctx', 'head'), perm)  22.6 us
    pallas_call x3, Pallas kernels, closing(): pl.pallas_call(kernel, out_shape=out_shape, in_specs=[SMEM, SMEM] + [VMEM...  16.6 us
    ppermute x9, starting transfers between devices, send(): return lax.ppermute(array, ('ctx', 'head'), perm)  16.4 us
    pallas_call x2, Pallas kernels, stage(): pl.pallas_call(kernel, out_shape=[jax.ShapeDtypeStruct((2,) + ACC, F32),...  11.7 us
    pallas_call x1, Pallas kernels, diagonal(): pl.pallas_call(diagonal_kernel, out_shape=[jax.ShapeDtypeStruct((QH, ROWS...  2.49 us
    unnamed x10, local copies, waits for them, and re-layouts  2.12 us
    pallas_call x1, Pallas kernels, packed_kv(): pl.pallas_call(pack_kernel, out_shape=jax.ShapeDtypeStruct((TOK, 2 * HD),...  1.91 us
  transfers between devices with their start and end apart: 9, of which 7 were waited for; matrix products, arithmetic and copies ran while one was open for 0% of the time, Pallas kernels for 37%

profile of v1, /device:TPU:68, one launch (start us, length us, event | category | flops | bytes accessed | tf_op | source)
XLA Modules:
  0.0 75.1 jit_solution(8335228431613605858)
XLA Ops:
  0.0 1.9 %pack_kv.1.kv_ref.refs_4_.refs_9_.refs_6_ = bf16[1024,256]{1,0:T(8,128)(2,1)} custom-call(bf16[1024,128]{1,0:T(8,128)(2,1)} %keys.1, bf16[1024,128]{1,0:T(8,128)(2,1)} %values.1), custom_call_target="tpu_custom_call" | custom-call | tf_op jit(solution)/shard_map/pack_kv/pallas_call | solution.py:320
  1.9 1.6 %collective-permute-start.3 = (bf16[1024,256]{1,0:T(8,128)(2,1)}, bf16[1024,256]{1,0:T(8,128)(2,1)S(1)}, u32[]{:S(2)}, u32[]{:S(2)}) collective-permute-start(bf16[1024,256]{1,0:T(8,128)(2,1)} %pack_kv.1.kv_ref.refs_4_.refs_9_.refs_6_), channel_id=1, source_target_pairs={{0,64},{1,193},{2,66},{3,195},{4,68},{5,197},{6,70},{7,199},{8,72}... | collective-permute-start | bytes 1572872 | tf_op jit(solution)/shard_map/ppermute | solution.py:51
  3.5 2.2 %collective-permute-start.2 = (bf16[1024,256]{1,0:T(8,128)(2,1)}, bf16[1024,256]{1,0:T(8,128)(2,1)S(1)}, u32[]{:S(2)}, u32[]{:S(2)}) collective-permute-start(bf16[1024,256]{1,0:T(8,128)(2,1)} %refs_2_.1), channel_id=1, source_target_pairs={{0,192},{1,65},{2,194},{3,67},{4,196},{5,69},{6,198},{7,71},{8,200... | collective-permute-start | bytes 1572872 | tf_op jit(solution)/shard_map/ppermute | solution.py:51
  5.7 4.5 %collective-permute-start = (bf16[1024,256]{1,0:T(8,128)(2,1)}, bf16[1024,256]{1,0:T(8,128)(2,1)S(1)}, u32[]{:S(2)}, u32[]{:S(2)}) collective-permute-start(bf16[1024,256]{1,0:T(8,128)(2,1)} %pack_kv.1.kv_ref.refs_4_.refs_9_.refs_6_), channel_id=1, source_target_pairs={{0,16},{1,49},{2,18},{3,51},{4,20},{5,53},{6,22},{7,55},{8,24},{9,... | collective-permute-start | bytes 1572872 | tf_op jit(solution)/shard_map/ppermute | solution.py:51
  10.2 1.1 %copy-done = bf16[1024,256]{1,0:T(8,128)(2,1)S(1)} copy-done((bf16[1024,256]{1,0:T(8,128)(2,1)S(1)}, bf16[1024,256]{1,0:T(8,128)(2,1)}, u32[]{:S(2)}) %copy-start) | copy-done | bytes 524312
  11.3 1.0 %copy-done.2 = bf16[1024,256]{1,0:T(8,128)(2,1)S(1)} copy-done((bf16[1024,256]{1,0:T(8,128)(2,1)S(1)}, bf16[1024,256]{1,0:T(8,128)(2,1)}, u32[]{:S(2)}) %copy-start.2) | copy-done | bytes 524312
  12.4 2.5 %diagonal.1 = (f32[2,136,1024]{2,1,0:T(8,128)S(1)}, f32[2,1,1024]{2,1,0:T(1,128)S(1)}) custom-call(bf16[1024,256]{1,0:T(8,128)(2,1)S(1)} %copy-done.2, bf16[1024,256]{1,0:T(8,128)(2,1)S(1)} %copy-done), custom_call_target="tpu_custom_call" | custom-call | flops 3221225472 | bytes 4194304 | tf_op jit(solution)/shard_map/diagonal/pallas_call | solution.py:90
  14.9 1.0 %collective-permute-done.3.refs_5_.refs_13_.refs_10_ = bf16[1024,256]{1,0:T(8,128)(2,1)S(1)} collective-permute-done((bf16[1024,256]{1,0:T(8,128)(2,1)}, bf16[1024,256]{1,0:T(8,128)(2,1)S(1)}, u32[]{:S(2)}, u32[]{:S(2)}) %collective-permute-start.3) | collective-permute-done | bytes 524320 | tf_op jit(solution)/shard_map/ppermute | solution.py:51
  15.8 1.2 %collective-permute-done.2.refs_2_ = bf16[1024,256]{1,0:T(8,128)(2,1)S(1)} collective-permute-done((bf16[1024,256]{1,0:T(8,128)(2,1)}, bf16[1024,256]{1,0:T(8,128)(2,1)S(1)}, u32[]{:S(2)}, u32[]{:S(2)}) %collective-permute-start.2) | collective-permute-done | bytes 524320 | tf_op jit(solution)/shard_map/ppermute | solution.py:51
  17.1 7.0 %stage.2 = (f32[2,2,136,1024]{3,2,1,0:T(8,128)S(1)}, f32[2,2,1,1024]{3,2,1,0:T(1,128)S(1)}) custom-call(s32[4]{0:T(128)S(1)} %pad_add_fusion.refs_0_, s32[16]{0:T(128)S(1)} %copy-done.4, bf16[1024,256]{1,0:T(8,128)(2,1)S(1)} %collective-permute-done.2.refs_2_, bf16[1024,256]{1,0:T(8,128)(2,1)S(1)} %copy-done.3, bf16[1024,256]{1,0:T(8,128)(2,1)S(1)} %copy-done.1, ...), custom_call_target="tpu_custom_call" | custom-call | flops 8589934592 | bytes 8388608 | tf_op jit(solution)/shard_map/stage/pallas_call | solution.py:171
  24.1 8.4 %collective-permute-done.1.refs_5_.refs_11_.refs_8_ = bf16[1024,256]{1,0:T(8,128)(2,1)S(1)} collective-permute-done((bf16[1024,256]{1,0:T(8,128)(2,1)}, bf16[1024,256]{1,0:T(8,128)(2,1)S(1)}, u32[]{:S(2)}, u32[]{:S(2)}) %collective-permute-start.1) | collective-permute-done | bytes 524320 | tf_op jit(solution)/shard_map/ppermute | solution.py:51
  32.5 2.6 %collective-permute-start.4 = (bf16[1024,256]{1,0:T(8,128)(2,1)S(1)}, bf16[1024,256]{1,0:T(8,128)(2,1)S(1)}, u32[]{:S(2)}, u32[]{:S(2)}) collective-permute-start(bf16[1024,256]{1,0:T(8,128)(2,1)S(1)} %collective-permute-done.refs_4_.refs_10_.refs_7_), channel_id=1, source_target_pairs={{0,16},{1,49},{2,18},{3,51},{4,20},{5,53},{6,22},{7,55},{8,24},{9,... | collective-permute-start | bytes 1572872 | tf_op jit(solution)/shard_map/ppermute | solution.py:51
  35.1 2.9 %collective-permute-start.5 = (bf16[1024,256]{1,0:T(8,128)(2,1)S(1)}, bf16[1024,256]{1,0:T(8,128)(2,1)S(1)}, u32[]{:S(2)}, u32[]{:S(2)}) collective-permute-start(bf16[1024,256]{1,0:T(8,128)(2,1)S(1)} %collective-permute-done.refs_4_.refs_10_.refs_7_), channel_id=1, source_target_pairs={{0,64},{1,193},{2,66},{3,195},{4,68},{5,197},{6,70},{7,199},{8,72}... | collective-permute-start | bytes 1572872 | tf_op jit(solution)/shard_map/ppermute | solution.py:51
  38.1 4.7 %stage.3 = (f32[2,2,136,1024]{3,2,1,0:T(8,128)S(1)}, f32[2,2,1,1024]{3,2,1,0:T(1,128)S(1)}) custom-call(s32[4]{0:T(128)S(1)} %pad_add_fusion.refs_0_, s32[16]{0:T(128)S(1)} %copy-done.4, bf16[1024,256]{1,0:T(8,128)(2,1)S(1)} %collective-permute-done.2.refs_2_, bf16[1024,256]{1,0:T(8,128)(2,1)S(1)} %copy-done.3, ...), custom_call_target="tpu_custom_call" | custom-call | flops 8589934592 | bytes 8388608 | tf_op jit(solution)/shard_map/stage/pallas_call | solution.py:171
  42.8 4.7 %collective-permute-done.4.refs_5_.refs_12_.refs_9_ = bf16[1024,256]{1,0:T(8,128)(2,1)S(1)} collective-permute-done((bf16[1024,256]{1,0:T(8,128)(2,1)S(1)}, bf16[1024,256]{1,0:T(8,128)(2,1)S(1)}, u32[]{:S(2)}, u32[]{:S(2)}) %collective-permute-start.4) | collective-permute-done | bytes 524320 | tf_op jit(solution)/shard_map/ppermute | solution.py:51
  47.5 3.3 %collective-permute-done.6.refs_4_.refs_15_.refs_12_ = bf16[1024,256]{1,0:T(8,128)(2,1)S(1)} collective-permute-done((bf16[1024,256]{1,0:T(8,128)(2,1)S(1)}, bf16[1024,256]{1,0:T(8,128)(2,1)S(1)}, u32[]{:S(2)}, u32[]{:S(2)}) %collective-permute-start.6) | collective-permute-done | bytes 524320 | tf_op jit(solution)/shard_map/ppermute | solution.py:51
  50.8 2.0 %collective-permute-start.7 = (bf16[1024,256]{1,0:T(8,128)(2,1)S(1)}, bf16[1024,256]{1,0:T(8,128)(2,1)S(1)}, u32[]{:S(2)}, u32[]{:S(2)}) collective-permute-start(bf16[1024,256]{1,0:T(8,128)(2,1)S(1)} %collective-permute-done.4.refs_5_.refs_12_.refs_9_), channel_id=1, source_target_pairs={{0,64},{1,193},{2,66},{3,195},{4,68},{5,197},{6,70},{7,199},{8,72}... | collective-permute-start | bytes 1572872 | tf_op jit(solution)/shard_map/ppermute | solution.py:51
  52.8 6.7 %guest.1 = (f32[1,2,136,1024]{3,2,1,0:T(8,128)S(1)}, f32[1,2,1,1024]{3,2,1,0:T(1,128)S(1)}) custom-call(s32[4]{0:T(128)S(1)} %pad_add_fusion.refs_0_, s32[16]{0:T(128)S(1)} %copy-done.4, bf16[1024,256]{1,0:T(8,128)(2,1)S(1)} %collective-permute-done.2.refs_2_, bf16[1024,256]{1,0:T(8,128)(2,1)S(1)} %collective-permute-done.5.refs_3_.refs_14_.refs_11_, ...), custom_call_target="tpu_custom_call" | custom-call | flops 6442450944 | bytes 8388608 | tf_op jit(solution)/shard_map/guest/pallas_call | solution.py:271
  59.6 0.4 collective-permute-done.7.refs_6_.refs_16_.refs_3_.refs_13_
  60.0 2.9 %away.1 = bf16[272,1024]{1,0:T(8,128)(2,1)S(1)} custom-call(s32[4]{0:T(128)S(1)} %pad_add_fusion.refs_0_, s32[16]{0:T(128)S(1)} %copy-done.4, bf16[1024,256]{1,0:T(8,128)(2,1)S(1)} %collective-permute-done.2.refs_2_, bf16[1024,256]{1,0:T(8,128)(2,1)S(1)} %collective-permute-done.7.refs_6_.refs_16_.refs_3_.refs_13_, ...), custom_call_target="tpu_custom_call" | custom-call | flops 2147483648 | bytes 8388608 | tf_op jit(solution)/shard_map/away/pallas_call | solution.py:271
  63.0 0.6 collective-permute-start.8
  63.6 6.9 %home.1 = (f32[1,2,136,1024]{3,2,1,0:T(8,128)S(1)}, f32[1,2,1,1024]{3,2,1,0:T(1,128)S(1)}) custom-call(s32[4]{0:T(128)S(1)} %pad_add_fusion.refs_0_, s32[16]{0:T(128)S(1)} %copy-done.4, bf16[1024,256]{1,0:T(8,128)(2,1)S(1)} %copy-done.3, bf16[1024,256]{1,0:T(8,128)(2,1)S(1)} %collective-permute-done.5.refs_3_.refs_14_.refs_11_, ...), custom_call_target="tpu_custom_call" | custom-call | flops 8589934592 | bytes 8388608 | tf_op jit(solution)/shard_map/home/pallas_call | solution.py:271
  70.5 3.5 %collective-permute-done.8.came = bf16[272,1024]{1,0:T(8,128)(2,1)S(1)} collective-permute-done((bf16[272,1024]{1,0:T(8,128)(2,1)S(1)}, bf16[272,1024]{1,0:T(8,128)(2,1)S(1)}, u32[]{:S(2)}, u32[]{:S(2)}) %collective-permute-start.8) | collective-permute-done | bytes 557088 | tf_op jit(solution)/shard_map/ppermute | solution.py:51
  74.0 1.1 %join.1 = bf16[1024,256]{1,0:T(8,128)(2,1)} custom-call(f32[1,2,136,1024]{3,2,1,0:T(8,128)S(1)} %get-tuple-element.34.acc, f32[1,2,1,1024]{3,2,1,0:T(1,128)S(1)} %get-tuple-element.35.shift, bf16[272,1024]{1,0:T(8,128)(2,1)S(1)} %collective-permute-done.8.came), custom_call_target="tpu_custom_call" | custom-call | tf_op jit(solution)/shard_map/join/pallas_call | solution.py:300
  (13 shorter events, 0.1 us)
Async XLA Ops:
  1.9 13.9 %collective-permute-start.3 = (bf16[1024,256]{1,0:T(8,128)(2,1)}, bf16[1024,256]{1,0:T(8,128)(2,1)S(1)}, u32[]{:S(2)}, u32[]{:S(2)}) collective-permute-start(bf16[1024,256]{1,0:T(8,128)(2,1)} %pack_kv.1.kv_ref.refs_4_.refs_9_.refs_6_), channel_id=1, source_target_pairs={{0,64},{1,193},{2,66},{3,195},{4,68},{5,197},{6,70},{7,199},{8,72}... | collective-permute-start | bytes 1572872 | tf_op jit(solution)/shard_map/ppermute | solution.py:51
  3.5 13.6 %collective-permute-start.2 = (bf16[1024,256]{1,0:T(8,128)(2,1)}, bf16[1024,256]{1,0:T(8,128)(2,1)S(1)}, u32[]{:S(2)}, u32[]{:S(2)}) collective-permute-start(bf16[1024,256]{1,0:T(8,128)(2,1)} %refs_2_.1), channel_id=1, source_target_pairs={{0,192},{1,65},{2,194},{3,67},{4,196},{5,69},{6,198},{7,71},{8,200... | collective-permute-start | bytes 1572872 | tf_op jit(solution)/shard_map/ppermute | solution.py:51
  5.7 18.4 %collective-permute-start = (bf16[1024,256]{1,0:T(8,128)(2,1)}, bf16[1024,256]{1,0:T(8,128)(2,1)S(1)}, u32[]{:S(2)}, u32[]{:S(2)}) collective-permute-start(bf16[1024,256]{1,0:T(8,128)(2,1)} %pack_kv.1.kv_ref.refs_4_.refs_9_.refs_6_), channel_id=1, source_target_pairs={{0,16},{1,49},{2,18},{3,51},{4,20},{5,53},{6,22},{7,55},{8,24},{9,... | collective-permute-start | bytes 1572872 | tf_op jit(solution)/shard_map/ppermute | solution.py:51
  10.2 22.4 %collective-permute-start.1 = (bf16[1024,256]{1,0:T(8,128)(2,1)}, bf16[1024,256]{1,0:T(8,128)(2,1)S(1)}, u32[]{:S(2)}, u32[]{:S(2)}) collective-permute-start(bf16[1024,256]{1,0:T(8,128)(2,1)} %pack_kv.1.kv_ref.refs_4_.refs_9_.refs_6_), channel_id=1, source_target_pairs={{0,48},{1,17},{2,50},{3,19},{4,52},{5,21},{6,54},{7,23},{8,56},{9,... | collective-permute-start | bytes 1572872 | tf_op jit(solution)/shard_map/ppermute | solution.py:51
  10.2 1.1 %copy-start = (bf16[1024,256]{1,0:T(8,128)(2,1)S(1)}, bf16[1024,256]{1,0:T(8,128)(2,1)}, u32[]{:S(2)}) copy-start(bf16[1024,256]{1,0:T(8,128)(2,1)} %pack_kv.1.kv_ref.refs_4_.refs_9_.refs_6_) | copy-start | bytes 1572868
  11.3 1.0 %copy-start.2 = (bf16[1024,256]{1,0:T(8,128)(2,1)S(1)}, bf16[1024,256]{1,0:T(8,128)(2,1)}, u32[]{:S(2)}) copy-start(bf16[1024,256]{1,0:T(8,128)(2,1)} %refs_2_.1) | copy-start | bytes 1572868
  12.3 4.7 %copy-start.1 = (bf16[1024,256]{1,0:T(8,128)(2,1)S(1)}, bf16[1024,256]{1,0:T(8,128)(2,1)}, u32[]{:S(2)}) copy-start(bf16[1024,256]{1,0:T(8,128)(2,1)} %pack_kv.1.kv_ref.refs_4_.refs_9_.refs_6_) | copy-start | bytes 1572868
  12.3 4.7 %copy-start.3 = (bf16[1024,256]{1,0:T(8,128)(2,1)S(1)}, bf16[1024,256]{1,0:T(8,128)(2,1)}, u32[]{:S(2)}) copy-start(bf16[1024,256]{1,0:T(8,128)(2,1)} %refs_2_.1) | copy-start | bytes 1572868
  12.3 4.7 %copy-start.4 = (s32[16]{0:T(128)S(1)}, s32[16]{0:T(128)}, u32[]{:S(2)}) copy-start(s32[16]{0:T(128)} %refs_1_.9) | copy-start | bytes 196
  32.5 15.0 %collective-permute-start.4 = (bf16[1024,256]{1,0:T(8,128)(2,1)S(1)}, bf16[1024,256]{1,0:T(8,128)(2,1)S(1)}, u32[]{:S(2)}, u32[]{:S(2)}) collective-permute-start(bf16[1024,256]{1,0:T(8,128)(2,1)S(1)} %collective-permute-done.refs_4_.refs_10_.refs_7_), channel_id=1, source_target_pairs={{0,16},{1,49},{2,18},{3,51},{4,20},{5,53},{6,22},{7,55},{8,24},{9,... | collective-permute-start | bytes 1572872 | tf_op jit(solution)/shard_map/ppermute | solution.py:51
  35.1 12.4 %collective-permute-start.5 = (bf16[1024,256]{1,0:T(8,128)(2,1)S(1)}, bf16[1024,256]{1,0:T(8,128)(2,1)S(1)}, u32[]{:S(2)}, u32[]{:S(2)}) collective-permute-start(bf16[1024,256]{1,0:T(8,128)(2,1)S(1)} %collective-permute-done.refs_4_.refs_10_.refs_7_), channel_id=1, source_target_pairs={{0,64},{1,193},{2,66},{3,195},{4,68},{5,197},{6,70},{7,199},{8,72}... | collective-permute-start | bytes 1572872 | tf_op jit(solution)/shard_map/ppermute | solution.py:51
  38.0 12.8 %collective-permute-start.6 = (bf16[1024,256]{1,0:T(8,128)(2,1)S(1)}, bf16[1024,256]{1,0:T(8,128)(2,1)S(1)}, u32[]{:S(2)}, u32[]{:S(2)}) collective-permute-start(bf16[1024,256]{1,0:T(8,128)(2,1)S(1)} %collective-permute-done.1.refs_5_.refs_11_.refs_8_), channel_id=1, source_target_pairs={{0,64},{1,193},{2,66},{3,195},{4,68},{5,197},{6,70},{7,199},{8,72}... | collective-permute-start | bytes 1572872 | tf_op jit(solution)/shard_map/ppermute | solution.py:51
  50.8 9.2 %collective-permute-start.7 = (bf16[1024,256]{1,0:T(8,128)(2,1)S(1)}, bf16[1024,256]{1,0:T(8,128)(2,1)S(1)}, u32[]{:S(2)}, u32[]{:S(2)}) collective-permute-start(bf16[1024,256]{1,0:T(8,128)(2,1)S(1)} %collective-permute-done.4.refs_5_.refs_12_.refs_9_), channel_id=1, source_target_pairs={{0,64},{1,193},{2,66},{3,195},{4,68},{5,197},{6,70},{7,199},{8,72}... | collective-permute-start | bytes 1572872 | tf_op jit(solution)/shard_map/ppermute | solution.py:51
  63.0 11.1 %collective-permute-start.8 = (bf16[272,1024]{1,0:T(8,128)(2,1)S(1)}, bf16[272,1024]{1,0:T(8,128)(2,1)S(1)}, u32[]{:S(2)}, u32[]{:S(2)}) collective-permute-start(bf16[272,1024]{1,0:T(8,128)(2,1)S(1)} %away.1), channel_id=1, source_target_pairs={{0,192},{1,65},{2,194},{3,67},{4,196},{5,69},{6,198},{7,71},{8,200... | collective-permute-start | bytes 1671176 | tf_op jit(solution)/shard_map/ppermute | solution.py:51

commit v2 on v1

--- a/solution.py
+++ b/solution.py
@@ -55,6 +55,12 @@
     return ref[:, h * HD:(h + 1) * HD]
 
 
+def fill_values(vt, kv_ref):
+    for n in range(TOK // HD):
+        tile = slice(n * HD, (n + 1) * HD)
+        vt[:HD, tile] = kv_ref[tile, HD:]
+
+
 def absorb(kb, vt, q_ref, acc, shift):
     scores = [dot_last(kb[...], head(q_ref, 0)), None]
     for h in range(QH):
@@ -75,7 +81,7 @@
 
 def diagonal_kernel(q_ref, kv_ref, acc, shift, vt):
     vt[HD:, :] = jnp.ones((8, TOK), BF16)
-    vt[:HD, :] = kv_ref[:, HD:].T
+    fill_values(vt, kv_ref)
     keys = lax.broadcasted_iota(jnp.int32, (TOK, TOK), 0)
     rows = lax.broadcasted_iota(jnp.int32, (TOK, TOK), 1)
     for h in range(QH):
@@ -126,7 +132,7 @@
                 @pl.when(n == place)
                 def _():
                     kb[...] = kv_refs[place][:, :HD]
-                    vt[:HD, :] = kv_refs[place][:, HD:].T
+                    fill_values(vt, kv_refs[place])
 
             def query(q):
                 @pl.when(flags[n * nq + q] > 0)
@@ -194,7 +200,7 @@
         def _():
             pltpu.sync_copy(source, buf)
             kb[...] = buf[:, :HD]
-            vt[:HD, :] = buf[:, HD:].T
+            fill_values(vt, buf)
 
             @pl.loop(0, 16)
             def _(tile):
@@ -307,13 +313,11 @@
     )(*state, came)
 
 
-def after(array, *others):
-    return lax.optimization_barrier((array,) + others)[0]
-
-
 def pack_kernel(keys, values, kv):
     kv[:, :HD] = keys[...]
-    kv[:, HD:] = values[...]
+    for n in range(TOK // HD):
+        tile = slice(n * HD, (n + 1) * HD)
+        kv[tile, HD:] = values[tile, :].T
 
 
 def packed_kv(keys, values):
@@ -340,22 +344,23 @@
     kv = packed_kv(keys, values)
     near_a = send(kv, forth)
     near_b = send(kv, back)
+    acc, shift = diagonal(q0, kv)
     mate_own = send(kv, key_perm)
     q1 = send(q0, query_perm)
-    state0 = diagonal(q0, kv)
     qs = [q1, q0]
-    state = stage(meta, order, qs, [kv, mate_own], [(0, OWN), (1, OWN)], [None, state0])
-
-    near_a, near_b = after((near_a, near_b), state[1])
+    state = stage(meta, order, qs, [kv, mate_own], [(0, OWN), (1, OWN)], [None, (acc, shift)])
+
+    near_a, near_b, shift = lax.optimization_barrier((near_a, near_b, state[1]))
     far = send(near_a, forth)
     mate_a = send(near_a, key_perm)
     mate_b = send(near_b, key_perm)
-    state = stage(meta, order, [q1, after(q0, near_a, near_b)], [near_a, near_b], [(0, NEAR_A), (0, NEAR_B)], state)
-
-    far, mate_a, mate_b = after((far, mate_a, mate_b), state[1])
+    state = stage(meta, order, qs, [near_a, near_b], [(0, NEAR_A), (0, NEAR_B)], [state[0], shift])
+
+    far, shift = lax.optimization_barrier((far, state[1]))
+    state = [state[0], shift]
     mate_far = send(far, key_perm)
     guest = closing(
-        meta, order, q1, 2, [after(mate_a, far), mate_b, far], [(1, NEAR_A), (1, NEAR_B), (0, FAR)], state, [], False
+        meta, order, q1, 2, [mate_a, mate_b, far], [(1, NEAR_A), (1, NEAR_B), (0, FAR)], state, [], False
     )
     everything = [kv, near_a, near_b, far, mate_own, mate_a, mate_b, mate_far]
     away = closing(meta, order, q1, 2, [mate_far], [(1, FAR)], guest, everything, True)

time: 74.7 us -> 73.1 us (0.979)
  the two profiles are of different devices: /device:TPU:68 before, /device:TPU:32 now
where the time goes in v2:
time: 73.1 us; the launch traced here: 72.6 us
  waiting for transfers between devices  39.3 us (54%)
  starting transfers between devices  16.8 us (23%)
  Pallas kernels  14.2 us (19%)
  local copies, waits for them, and re-layouts  2.09 us (3%)
    ppermute x9, waiting for transfers between devices, send(): return lax.ppermute(array, ('ctx', 'head'), perm)  39.3 us
    ppermute x9, starting transfers between devices, send(): return lax.ppermute(array, ('ctx', 'head'), perm)  16.8 us
    pallas_call x2, Pallas kernels, stage(): pl.pallas_call(kernel, out_shape=[jax.ShapeDtypeStruct((2,) + ACC, F32),...  5.9 us
    pallas_call x3, Pallas kernels, closing(): pl.pallas_call(kernel, out_shape=out_shape, in_specs=[SMEM, SMEM] + [VMEM...  2.69 us
    pallas_call x1, Pallas kernels, diagonal(): pl.pallas_call(diagonal_kernel, out_shape=[jax.ShapeDtypeStruct((QH, ROWS...  2.5 us
    unnamed x10, local copies, waits for them, and re-layouts  2.09 us
    pallas_call x1, Pallas kernels, packed_kv(): pl.pallas_call(pack_kernel, out_shape=jax.ShapeDtypeStruct((TOK, 2 * HD),...  1.94 us
  transfers between devices with their start and end apart: 9, of which 6 were waited for; matrix products, arithmetic and copies ran while one was open for 0% of the time, Pallas kernels for 14%

profile of v2, /device:TPU:32, one launch (start us, length us, event | category | flops | bytes accessed | tf_op | source)
XLA Modules:
  0.0 72.6 jit_solution(11149133557452354981)
XLA Ops:
  0.0 1.9 %pack_kv.1.kv_ref.refs_4_.refs_9_.refs_6_ = bf16[1024,256]{1,0:T(8,128)(2,1)} custom-call(bf16[1024,128]{1,0:T(8,128)(2,1)} %keys.1, bf16[1024,128]{1,0:T(8,128)(2,1)} %values.1), custom_call_target="tpu_custom_call" | custom-call | tf_op jit(solution)/shard_map/pack_kv/pallas_call | solution.py:324
  1.9 1.6 %collective-permute-start.3 = (bf16[1024,256]{1,0:T(8,128)(2,1)}, bf16[1024,256]{1,0:T(8,128)(2,1)S(1)}, u32[]{:S(2)}, u32[]{:S(2)}) collective-permute-start(bf16[1024,256]{1,0:T(8,128)(2,1)} %pack_kv.1.kv_ref.refs_4_.refs_9_.refs_6_), channel_id=1, source_target_pairs={{0,64},{1,193},{2,66},{3,195},{4,68},{5,197},{6,70},{7,199},{8,72}... | collective-permute-start | bytes 1572872 | tf_op jit(solution)/shard_map/ppermute | solution.py:51
  3.5 2.2 %collective-permute-start.2 = (bf16[1024,256]{1,0:T(8,128)(2,1)}, bf16[1024,256]{1,0:T(8,128)(2,1)S(1)}, u32[]{:S(2)}, u32[]{:S(2)}) collective-permute-start(bf16[1024,256]{1,0:T(8,128)(2,1)} %refs_2_.1), channel_id=1, source_target_pairs={{0,192},{1,65},{2,194},{3,67},{4,196},{5,69},{6,198},{7,71},{8,200... | collective-permute-start | bytes 1572872 | tf_op jit(solution)/shard_map/ppermute | solution.py:51
  5.7 3.3 %collective-permute-start = (bf16[1024,256]{1,0:T(8,128)(2,1)}, bf16[1024,256]{1,0:T(8,128)(2,1)S(1)}, u32[]{:S(2)}, u32[]{:S(2)}) collective-permute-start(bf16[1024,256]{1,0:T(8,128)(2,1)} %pack_kv.1.kv_ref.refs_4_.refs_9_.refs_6_), channel_id=1, source_target_pairs={{0,16},{1,49},{2,18},{3,51},{4,20},{5,53},{6,22},{7,55},{8,24},{9,... | collective-permute-start | bytes 1572872 | tf_op jit(solution)/shard_map/ppermute | solution.py:51
  9.0 2.1 %collective-permute-start.1 = (bf16[1024,256]{1,0:T(8,128)(2,1)}, bf16[1024,256]{1,0:T(8,128)(2,1)S(1)}, u32[]{:S(2)}, u32[]{:S(2)}) collective-permute-start(bf16[1024,256]{1,0:T(8,128)(2,1)} %pack_kv.1.kv_ref.refs_4_.refs_9_.refs_6_), channel_id=1, source_target_pairs={{0,48},{1,17},{2,50},{3,19},{4,52},{5,21},{6,54},{7,23},{8,56},{9,... | collective-permute-start | bytes 1572872 | tf_op jit(solution)/shard_map/ppermute | solution.py:51
  11.2 1.0 %copy-done = bf16[1024,256]{1,0:T(8,128)(2,1)S(1)} copy-done((bf16[1024,256]{1,0:T(8,128)(2,1)S(1)}, bf16[1024,256]{1,0:T(8,128)(2,1)}, u32[]{:S(2)}) %copy-start) | copy-done | bytes 524312
  12.2 1.0 %copy-done.2 = bf16[1024,256]{1,0:T(8,128)(2,1)S(1)} copy-done((bf16[1024,256]{1,0:T(8,128)(2,1)S(1)}, bf16[1024,256]{1,0:T(8,128)(2,1)}, u32[]{:S(2)}) %copy-start.2) | copy-done | bytes 524312
  13.3 2.5 %diagonal.1 = (f32[2,136,1024]{2,1,0:T(8,128)S(1)}, f32[2,1,1024]{2,1,0:T(1,128)S(1)}) custom-call(bf16[1024,256]{1,0:T(8,128)(2,1)S(1)} %copy-done.2, bf16[1024,256]{1,0:T(8,128)(2,1)S(1)} %copy-done), custom_call_target="tpu_custom_call" | custom-call | flops 3221225472 | bytes 4194304 | tf_op jit(solution)/shard_map/diagonal/pallas_call | solution.py:96
  15.8 1.2 %collective-permute-done.2.refs_2_ = bf16[1024,256]{1,0:T(8,128)(2,1)S(1)} collective-permute-done((bf16[1024,256]{1,0:T(8,128)(2,1)}, bf16[1024,256]{1,0:T(8,128)(2,1)S(1)}, u32[]{:S(2)}, u32[]{:S(2)}) %collective-permute-start.2) | collective-permute-done | bytes 524320 | tf_op jit(solution)/shard_map/ppermute | solution.py:51
  17.1 5.1 %stage.2 = (f32[2,2,136,1024]{3,2,1,0:T(8,128)S(1)}, f32[2,2,1,1024]{3,2,1,0:T(1,128)S(1)}) custom-call(s32[4]{0:T(128)S(1)} %pad_add_fusion.refs_0_, s32[16]{0:T(128)S(1)} %copy-done.4, bf16[1024,256]{1,0:T(8,128)(2,1)S(1)} %collective-permute-done.2.refs_2_, bf16[1024,256]{1,0:T(8,128)(2,1)S(1)} %copy-done.3, bf16[1024,256]{1,0:T(8,128)(2,1)S(1)} %copy-done.1, ...), custom_call_target="tpu_custom_call" | custom-call | flops 8589934592 | bytes 8388608 | tf_op jit(solution)/shard_map/stage/pallas_call | solution.py:177
  22.2 12.4 %collective-permute-done.refs_4_.refs_10_.refs_7_ = bf16[1024,256]{1,0:T(8,128)(2,1)S(1)} collective-permute-done((bf16[1024,256]{1,0:T(8,128)(2,1)}, bf16[1024,256]{1,0:T(8,128)(2,1)S(1)}, u32[]{:S(2)}, u32[]{:S(2)}) %collective-permute-start) | collective-permute-done | bytes 524320 | tf_op jit(solution)/shard_map/ppermute | solution.py:51
  34.6 1.1 %collective-permute-start.6 = (bf16[1024,256]{1,0:T(8,128)(2,1)S(1)}, bf16[1024,256]{1,0:T(8,128)(2,1)S(1)}, u32[]{:S(2)}, u32[]{:S(2)}) collective-permute-start(bf16[1024,256]{1,0:T(8,128)(2,1)S(1)} %collective-permute-done.refs_4_.refs_10_.refs_7_), channel_id=1, source_target_pairs={{0,16},{1,49},{2,18},{3,51},{4,20},{5,53},{6,22},{7,55},{8,24},{9,... | collective-permute-start | bytes 1572872 | tf_op jit(solution)/shard_map/ppermute | solution.py:51
  35.7 0.7 collective-permute-start.4
  36.3 1.3 %collective-permute-start.5 = (bf16[1024,256]{1,0:T(8,128)(2,1)S(1)}, bf16[1024,256]{1,0:T(8,128)(2,1)S(1)}, u32[]{:S(2)}, u32[]{:S(2)}) collective-permute-start(bf16[1024,256]{1,0:T(8,128)(2,1)S(1)} %collective-permute-done.1.refs_5_.refs_11_.refs_8_), channel_id=1, source_target_pairs={{0,64},{1,193},{2,66},{3,195},{4,68},{5,197},{6,70},{7,199},{8,72}... | collective-permute-start | bytes 1572872 | tf_op jit(solution)/shard_map/ppermute | solution.py:51
  37.7 0.8 %stage.3 = (f32[2,2,136,1024]{3,2,1,0:T(8,128)S(1)}, f32[2,2,1,1024]{3,2,1,0:T(1,128)S(1)}) custom-call(s32[4]{0:T(128)S(1)} %pad_add_fusion.refs_0_, s32[16]{0:T(128)S(1)} %copy-done.4, bf16[1024,256]{1,0:T(8,128)(2,1)S(1)} %collective-permute-done.2.refs_2_, bf16[1024,256]{1,0:T(8,128)(2,1)S(1)} %copy-done.3, ...), custom_call_target="tpu_custom_call" | custom-call | flops 8589934592 | bytes 8388608 | tf_op jit(solution)/shard_map/stage/pallas_call | solution.py:177
  38.5 12.0 %collective-permute-done.6.refs_5_.refs_12_.refs_9_ = bf16[1024,256]{1,0:T(8,128)(2,1)S(1)} collective-permute-done((bf16[1024,256]{1,0:T(8,128)(2,1)S(1)}, bf16[1024,256]{1,0:T(8,128)(2,1)S(1)}, u32[]{:S(2)}, u32[]{:S(2)}) %collective-permute-start.6) | collective-permute-done | bytes 524320 | tf_op jit(solution)/shard_map/ppermute | solution.py:51
  50.5 1.5 %collective-permute-start.7 = (bf16[1024,256]{1,0:T(8,128)(2,1)S(1)}, bf16[1024,256]{1,0:T(8,128)(2,1)S(1)}, u32[]{:S(2)}, u32[]{:S(2)}) collective-permute-start(bf16[1024,256]{1,0:T(8,128)(2,1)S(1)} %collective-permute-done.6.refs_5_.refs_12_.refs_9_), channel_id=1, source_target_pairs={{0,64},{1,193},{2,66},{3,195},{4,68},{5,197},{6,70},{7,199},{8,72}... | collective-permute-start | bytes 1572872 | tf_op jit(solution)/shard_map/ppermute | solution.py:51
  52.1 0.7 guest.1
  52.8 6.9 %collective-permute-done.7.refs_6_.refs_16_.refs_3_.refs_13_ = bf16[1024,256]{1,0:T(8,128)(2,1)S(1)} collective-permute-done((bf16[1024,256]{1,0:T(8,128)(2,1)S(1)}, bf16[1024,256]{1,0:T(8,128)(2,1)S(1)}, u32[]{:S(2)}, u32[]{:S(2)}) %collective-permute-start.7) | collective-permute-done | bytes 524320 | tf_op jit(solution)/shard_map/ppermute | solution.py:51
  59.7 0.9 %away.1 = bf16[272,1024]{1,0:T(8,128)(2,1)S(1)} custom-call(s32[4]{0:T(128)S(1)} %pad_add_fusion.refs_0_, s32[16]{0:T(128)S(1)} %copy-done.4, bf16[1024,256]{1,0:T(8,128)(2,1)S(1)} %collective-permute-done.2.refs_2_, bf16[1024,256]{1,0:T(8,128)(2,1)S(1)} %collective-permute-done.7.refs_6_.refs_16_.refs_3_.refs_13_, ...), custom_call_target="tpu_custom_call" | custom-call | flops 2147483648 | bytes 8388608 | tf_op jit(solution)/shard_map/away/pallas_call | solution.py:277
  60.6 3.0 %collective-permute-start.8 = (bf16[272,1024]{1,0:T(8,128)(2,1)S(1)}, bf16[272,1024]{1,0:T(8,128)(2,1)S(1)}, u32[]{:S(2)}, u32[]{:S(2)}) collective-permute-start(bf16[272,1024]{1,0:T(8,128)(2,1)S(1)} %away.1), channel_id=1, source_target_pairs={{0,192},{1,65},{2,194},{3,67},{4,196},{5,69},{6,198},{7,71},{8,200... | collective-permute-start | bytes 1671176 | tf_op jit(solution)/shard_map/ppermute | solution.py:51
  63.6 1.1 %home.1 = (f32[1,2,136,1024]{3,2,1,0:T(8,128)S(1)}, f32[1,2,1,1024]{3,2,1,0:T(1,128)S(1)}) custom-call(s32[4]{0:T(128)S(1)} %pad_add_fusion.refs_0_, s32[16]{0:T(128)S(1)} %copy-done.4, bf16[1024,256]{1,0:T(8,128)(2,1)S(1)} %copy-done.3, bf16[1024,256]{1,0:T(8,128)(2,1)S(1)} %collective-permute-done.4.refs_3_.refs_14_.refs_11_, ...), custom_call_target="tpu_custom_call" | custom-call | flops 8589934592 | bytes 8388608 | tf_op jit(solution)/shard_map/home/pallas_call | solution.py:277
  64.8 6.7 %collective-permute-done.8.came = bf16[272,1024]{1,0:T(8,128)(2,1)S(1)} collective-permute-done((bf16[272,1024]{1,0:T(8,128)(2,1)S(1)}, bf16[272,1024]{1,0:T(8,128)(2,1)S(1)}, u32[]{:S(2)}, u32[]{:S(2)}) %collective-permute-start.8) | collective-permute-done | bytes 557088 | tf_op jit(solution)/shard_map/ppermute | solution.py:51
  71.4 1.1 %join.1 = bf16[1024,256]{1,0:T(8,128)(2,1)} custom-call(f32[1,2,136,1024]{3,2,1,0:T(8,128)S(1)} %get-tuple-element.31.acc, f32[1,2,1,1024]{3,2,1,0:T(1,128)S(1)} %get-tuple-element.32.shift, bf16[272,1024]{1,0:T(8,128)(2,1)S(1)} %collective-permute-done.8.came), custom_call_target="tpu_custom_call" | custom-call | tf_op jit(solution)/shard_map/join/pallas_call | solution.py:306
  (13 shorter events, 0.2 us)
Async XLA Ops:
  1.9 13.9 %collective-permute-start.3 = (bf16[1024,256]{1,0:T(8,128)(2,1)}, bf16[1024,256]{1,0:T(8,128)(2,1)S(1)}, u32[]{:S(2)}, u32[]{:S(2)}) collective-permute-start(bf16[1024,256]{1,0:T(8,128)(2,1)} %pack_kv.1.kv_ref.refs_4_.refs_9_.refs_6_), channel_id=1, source_target_pairs={{0,64},{1,193},{2,66},{3,195},{4,68},{5,197},{6,70},{7,199},{8,72}... | collective-permute-start | bytes 1572872 | tf_op jit(solution)/shard_map/ppermute | solution.py:51
  3.5 13.6 %collective-permute-start.2 = (bf16[1024,256]{1,0:T(8,128)(2,1)}, bf16[1024,256]{1,0:T(8,128)(2,1)S(1)}, u32[]{:S(2)}, u32[]{:S(2)}) collective-permute-start(bf16[1024,256]{1,0:T(8,128)(2,1)} %refs_2_.1), channel_id=1, source_target_pairs={{0,192},{1,65},{2,194},{3,67},{4,196},{5,69},{6,198},{7,71},{8,200... | collective-permute-start | bytes 1572872 | tf_op jit(solution)/shard_map/ppermute | solution.py:51
  5.7 28.9 %collective-permute-start = (bf16[1024,256]{1,0:T(8,128)(2,1)}, bf16[1024,256]{1,0:T(8,128)(2,1)S(1)}, u32[]{:S(2)}, u32[]{:S(2)}) collective-permute-start(bf16[1024,256]{1,0:T(8,128)(2,1)} %pack_kv.1.kv_ref.refs_4_.refs_9_.refs_6_), channel_id=1, source_target_pairs={{0,16},{1,49},{2,18},{3,51},{4,20},{5,53},{6,22},{7,55},{8,24},{9,... | collective-permute-start | bytes 1572872 | tf_op jit(solution)/shard_map/ppermute | solution.py:51
  9.0 25.6 %collective-permute-start.1 = (bf16[1024,256]{1,0:T(8,128)(2,1)}, bf16[1024,256]{1,0:T(8,128)(2,1)S(1)}, u32[]{:S(2)}, u32[]{:S(2)}) collective-permute-start(bf16[1024,256]{1,0:T(8,128)(2,1)} %pack_kv.1.kv_ref.refs_4_.refs_9_.refs_6_), channel_id=1, source_target_pairs={{0,48},{1,17},{2,50},{3,19},{4,52},{5,21},{6,54},{7,23},{8,56},{9,... | collective-permute-start | bytes 1572872 | tf_op jit(solution)/shard_map/ppermute | solution.py:51
  11.2 1.0 %copy-start = (bf16[1024,256]{1,0:T(8,128)(2,1)S(1)}, bf16[1024,256]{1,0:T(8,128)(2,1)}, u32[]{:S(2)}) copy-start(bf16[1024,256]{1,0:T(8,128)(2,1)} %pack_kv.1.kv_ref.refs_4_.refs_9_.refs_6_) | copy-start | bytes 1572868
  12.2 1.0 %copy-start.2 = (bf16[1024,256]{1,0:T(8,128)(2,1)S(1)}, bf16[1024,256]{1,0:T(8,128)(2,1)}, u32[]{:S(2)}) copy-start(bf16[1024,256]{1,0:T(8,128)(2,1)} %refs_2_.1) | copy-start | bytes 1572868
  13.3 3.8 %copy-start.1 = (bf16[1024,256]{1,0:T(8,128)(2,1)S(1)}, bf16[1024,256]{1,0:T(8,128)(2,1)}, u32[]{:S(2)}) copy-start(bf16[1024,256]{1,0:T(8,128)(2,1)} %pack_kv.1.kv_ref.refs_4_.refs_9_.refs_6_) | copy-start | bytes 1572868
  13.3 3.8 %copy-start.3 = (bf16[1024,256]{1,0:T(8,128)(2,1)S(1)}, bf16[1024,256]{1,0:T(8,128)(2,1)}, u32[]{:S(2)}) copy-start(bf16[1024,256]{1,0:T(8,128)(2,1)} %refs_2_.1) | copy-start | bytes 1572868
  13.3 3.8 %copy-start.4 = (s32[16]{0:T(128)S(1)}, s32[16]{0:T(128)}, u32[]{:S(2)}) copy-start(s32[16]{0:T(128)} %refs_1_.9) | copy-start | bytes 196
  34.6 15.9 %collective-permute-start.6 = (bf16[1024,256]{1,0:T(8,128)(2,1)S(1)}, bf16[1024,256]{1,0:T(8,128)(2,1)S(1)}, u32[]{:S(2)}, u32[]{:S(2)}) collective-permute-start(bf16[1024,256]{1,0:T(8,128)(2,1)S(1)} %collective-permute-done.refs_4_.refs_10_.refs_7_), channel_id=1, source_target_pairs={{0,16},{1,49},{2,18},{3,51},{4,20},{5,53},{6,22},{7,55},{8,24},{9,... | collective-permute-start | bytes 1572872 | tf_op jit(solution)/shard_map/ppermute | solution.py:51
  35.7 16.4 %collective-permute-start.4 = (bf16[1024,256]{1,0:T(8,128)(2,1)S(1)}, bf16[1024,256]{1,0:T(8,128)(2,1)S(1)}, u32[]{:S(2)}, u32[]{:S(2)}) collective-permute-start(bf16[1024,256]{1,0:T(8,128)(2,1)S(1)} %collective-permute-done.refs_4_.refs_10_.refs_7_), channel_id=1, source_target_pairs={{0,64},{1,193},{2,66},{3,195},{4,68},{5,197},{6,70},{7,199},{8,72}... | collective-permute-start | bytes 1572872 | tf_op jit(solution)/shard_map/ppermute | solution.py:51
  36.3 15.7 %collective-permute-start.5 = (bf16[1024,256]{1,0:T(8,128)(2,1)S(1)}, bf16[1024,256]{1,0:T(8,128)(2,1)S(1)}, u32[]{:S(2)}, u32[]{:S(2)}) collective-permute-start(bf16[1024,256]{1,0:T(8,128)(2,1)S(1)} %collective-permute-done.1.refs_5_.refs_11_.refs_8_), channel_id=1, source_target_pairs={{0,64},{1,193},{2,66},{3,195},{4,68},{5,197},{6,70},{7,199},{8,72}... | collective-permute-start | bytes 1572872 | tf_op jit(solution)/shard_map/ppermute | solution.py:51
  50.5 9.2 %collective-permute-start.7 = (bf16[1024,256]{1,0:T(8,128)(2,1)S(1)}, bf16[1024,256]{1,0:T(8,128)(2,1)S(1)}, u32[]{:S(2)}, u32[]{:S(2)}) collective-permute-start(bf16[1024,256]{1,0:T(8,128)(2,1)S(1)} %collective-permute-done.6.refs_5_.refs_12_.refs_9_), channel_id=1, source_target_pairs={{0,64},{1,193},{2,66},{3,195},{4,68},{5,197},{6,70},{7,199},{8,72}... | collective-permute-start | bytes 1572872 | tf_op jit(solution)/shard_map/ppermute | solution.py:51
  60.6 10.8 %collective-permute-start.8 = (bf16[272,1024]{1,0:T(8,128)(2,1)S(1)}, bf16[272,1024]{1,0:T(8,128)(2,1)S(1)}, u32[]{:S(2)}, u32[]{:S(2)}) collective-permute-start(bf16[272,1024]{1,0:T(8,128)(2,1)S(1)} %away.1), channel_id=1, source_target_pairs={{0,192},{1,65},{2,194},{3,67},{4,196},{5,69},{6,198},{7,71},{8,200... | collective-permute-start | bytes 1671176 | tf_op jit(solution)/shard_map/ppermute | solution.py:51

commit v3 on v2

--- a/solution.py
+++ b/solution.py
@@ -8,6 +8,7 @@
 HD = 128
 QH = 2
 TOK = 1024
+HALF = TOK // 2
 ROWS = HD + 8
 SCALE = 168.0 ** (-0.5) * 1.4426950408889634
 VMEM = pl.BlockSpec(memory_space=pltpu.VMEM)
@@ -56,7 +57,7 @@
 
 
 def fill_values(vt, kv_ref):
-    for n in range(TOK // HD):
+    for n in range(kv_ref.shape[0] // HD):
         tile = slice(n * HD, (n + 1) * HD)
         vt[:HD, tile] = kv_ref[tile, HD:]
 
@@ -110,12 +111,21 @@
 
 ACC = (QH, ROWS, TOK)
 SHIFT = (QH, 1, TOK)
-SCRATCH = [pltpu.VMEM((TOK, HD), BF16), pltpu.VMEM((ROWS, TOK), BF16), pltpu.SMEM((16,), jnp.int32)]
+SCRATCH = [pltpu.VMEM((HALF, HD), BF16), pltpu.VMEM((ROWS, HALF), BF16), pltpu.SMEM((32,), jnp.int32)]
+
+
+def halves(refs):
+    parts = []
+    for ref in refs:
+        parts += [ref] if ref.shape[0] == HALF else [ref.at[:HALF], ref.at[HALF:]]
+    return parts
 
 
 def run_units(meta, order, q_refs, q_ids, kv_refs, blocks, accs, shifts, kb, vt, flags):
+    kv_refs = halves(kv_refs)
     nq, nb = len(q_ids), len(blocks)
-    vt[HD:, :] = jnp.ones((8, TOK), BF16)
+    assert len(kv_refs) == nb
+    vt[HD:, :] = jnp.ones((8, HALF), BF16)
     for n, block in enumerate(blocks):
         rank = rank_of(meta, order, *block)
         for q, q_id in enumerate(q_ids):
@@ -182,19 +192,19 @@
         scratch_shapes=[pltpu.VMEM((2, TOK, QH * HD), BF16)] + SCRATCH,
         compiler_params=pltpu.CompilerParams(vmem_limit_bytes=32 << 20),
         cost_estimate=pl.CostEstimate(
-            flops=2 * len(blocks) << 31, bytes_accessed=8 << 20, transcendentals=2 * len(blocks) << 21
+            flops=2 * len(blocks) << 30, bytes_accessed=8 << 20, transcendentals=2 * len(blocks) << 20
         ),
         name="stage",
     )(meta, order, *qs, *kvs, *old)
 
 
-def recompute(meta, order, q_id, q_ref, sources, acc, shift, buf, kb, vt):
+def recompute(meta, order, q_id, q_ref, sources, acc, shift, kb, vt, buf):
     query_rank = order[meta[q_id]]
     acc[0] = jnp.zeros(ACC, F32)
     shift[0] = jnp.full(SHIFT, -1e30, F32)
 
-    for n, source in enumerate(sources):
-        rank = rank_of(meta, order, n // 4, n % 4)
+    for n, source in enumerate(halves(sources)):
+        rank = rank_of(meta, order, n // 8, n // 2 % 4)
 
         @pl.when(rank <= query_rank)
         def _():
@@ -206,8 +216,8 @@
             def _(tile):
                 h, start = tile & 1, pl.multiple_of((tile >> 1) * HD, HD)
                 cols = pl.ds(start, HD)
-                keys = lax.broadcasted_iota(jnp.int32, (TOK, HD), 0) + rank * TOK
-                rows = lax.broadcasted_iota(jnp.int32, (TOK, HD), 1) + query_rank * TOK + start
+                keys = lax.broadcasted_iota(jnp.int32, (HALF, HD), 0) + (rank * TOK + n % 2 * HALF)
+                rows = lax.broadcasted_iota(jnp.int32, (HALF, HD), 1) + query_rank * TOK + start
                 query = q_ref[cols, pl.ds(pl.multiple_of(h * HD, HD), HD)]
                 scores = dot_last(kb[...], query) * SCALE
                 scores = jnp.where(keys <= rows, scores, -jnp.inf)
@@ -249,7 +259,7 @@
 
         @pl.when(jnp.logical_and(active > 0, faults > 0.0))
         def _():
-            recompute(meta_ref, order_ref, q_id, q_ref, all_refs, acc, shift, buf, kb, vt)
+            recompute(meta_ref, order_ref, q_id, q_ref, all_refs, acc, shift, kb, vt, buf)
 
         if pack:
             for h in range(QH):
@@ -266,7 +276,7 @@
                 sent[QH * HD + 8 * h:QH * HD + 8 * h + 8, :] = packed.astype(BF16)
 
     state_shapes = [((1,) + ACC, F32), ((1,) + SHIFT, F32)]
-    scratch = [pltpu.VMEM((TOK, 2 * HD), BF16), pltpu.VMEM((1, TOK, QH * HD), BF16)] + SCRATCH
+    scratch = [pltpu.VMEM((HALF, 2 * HD), BF16), pltpu.VMEM((1, TOK, QH * HD), BF16)] + SCRATCH
     if pack:
         out_shape = jax.ShapeDtypeStruct((QH * HD + 16, TOK), BF16)
         out_specs = VMEM
@@ -282,7 +292,7 @@
         scratch_shapes=scratch,
         compiler_params=pltpu.CompilerParams(vmem_limit_bytes=32 << 20),
         cost_estimate=pl.CostEstimate(
-            flops=len(blocks) << 31, bytes_accessed=8 << 20, transcendentals=len(blocks) << 21
+            flops=len(blocks) << 30, bytes_accessed=8 << 20, transcendentals=len(blocks) << 20
         ),
         name="away" if pack else "home" if ne else "guest",
     )(meta, order, q, *kvs, *state, *everything)
@@ -313,19 +323,23 @@
     )(*state, came)
 
 
-def pack_kernel(keys, values, kv):
-    kv[:, :HD] = keys[...]
+def pack_kernel(keys, values, kv, kv_low, kv_high):
     for n in range(TOK // HD):
         tile = slice(n * HD, (n + 1) * HD)
-        kv[tile, HD:] = values[tile, :].T
+        part = (kv_low, kv_high)[n * HD // HALF]
+        at = slice(n * HD % HALF, n * HD % HALF + HD)
+        turned = values[tile, :].T
+        for out, place in ((kv, tile), (part, at)):
+            out[place, :HD] = keys[tile, :]
+            out[place, HD:] = turned
 
 
 def packed_kv(keys, values):
     return pl.pallas_call(
         pack_kernel,
-        out_shape=jax.ShapeDtypeStruct((TOK, 2 * HD), BF16),
+        out_shape=[jax.ShapeDtypeStruct((rows, 2 * HD), BF16) for rows in (TOK, HALF, HALF)],
         in_specs=[VMEM] * 2,
-        out_specs=VMEM,
+        out_specs=[VMEM] * 3,
         name="pack_kv",
     )(keys, values)
 
@@ -341,34 +355,43 @@
 
     key_perm, query_perm = mate_perm(key_mate), mate_perm(query_mate)
     forth, back = ring_perm(1), ring_perm(-1)
-    kv = packed_kv(keys, values)
-    near_a = send(kv, forth)
-    near_b = send(kv, back)
-    acc, shift = diagonal(q0, kv)
+    kv, kv_low, kv_high = packed_kv(keys, values)
+    a_low, b_low = send(kv_low, forth), send(kv_low, back)
     mate_own = send(kv, key_perm)
     q1 = send(q0, query_perm)
+    a_high, b_high = send(kv_high, forth), send(kv_high, back)
+    state0 = diagonal(q0, kv)
+
+    far_low = send(a_low, forth)
+    mate_a_low, mate_b_low = send(a_low, key_perm), send(b_low, key_perm)
     qs = [q1, q0]
-    state = stage(meta, order, qs, [kv, mate_own], [(0, OWN), (1, OWN)], [None, (acc, shift)])
-
-    near_a, near_b, shift = lax.optimization_barrier((near_a, near_b, state[1]))
-    far = send(near_a, forth)
-    mate_a = send(near_a, key_perm)
-    mate_b = send(near_b, key_perm)
-    state = stage(meta, order, qs, [near_a, near_b], [(0, NEAR_A), (0, NEAR_B)], [state[0], shift])
-
-    far, shift = lax.optimization_barrier((far, state[1]))
+    state = stage(
+        meta, order, qs, [kv, mate_own, a_low, b_low],
+        [(0, OWN), (0, OWN), (1, OWN), (1, OWN), (0, NEAR_A), (0, NEAR_B)], [None, state0],
+    )
+
+    a_high, b_high, shift = lax.optimization_barrier((a_high, b_high, state[1]))
+    far_high = send(a_high, forth)
+    mate_a_high, mate_b_high = send(a_high, key_perm), send(b_high, key_perm)
+    state = stage(
+        meta, order, qs, [a_high, b_high, mate_a_low, mate_b_low],
+        [(0, NEAR_A), (0, NEAR_B), (1, NEAR_A), (1, NEAR_B)], [state[0], shift],
+    )
+
+    far_low, far_high, shift = lax.optimization_barrier((far_low, far_high, state[1]))
     state = [state[0], shift]
-    mate_far = send(far, key_perm)
-    guest = closing(
-        meta, order, q1, 2, [mate_a, mate_b, far], [(1, NEAR_A), (1, NEAR_B), (0, FAR)], state, [], False
-    )
-    everything = [kv, near_a, near_b, far, mate_own, mate_a, mate_b, mate_far]
-    away = closing(meta, order, q1, 2, [mate_far], [(1, FAR)], guest, everything, True)
+    mate_far_low, mate_far_high = send(far_low, key_perm), send(far_high, key_perm)
+    late = [mate_a_high, mate_b_high, far_low, far_high]
+    late_blocks = [(1, NEAR_A), (1, NEAR_B), (0, FAR), (0, FAR)]
+    guest = closing(meta, order, q1, 2, late, late_blocks, state, [], False)
+    everything = [
+        kv, a_low, a_high, b_low, b_high, far_low, far_high,
+        mate_own, mate_a_low, mate_a_high, mate_b_low, mate_b_high, mate_far_low, mate_far_high,
+    ]
+    last, last_blocks = [mate_far_low, mate_far_high], [(1, FAR), (1, FAR)]
+    away = closing(meta, order, q1, 2, last, last_blocks, guest, everything, True)
     came = send(away, query_perm)
-    own = closing(
-        meta, order, q0, 0, [mate_a, mate_b, far, mate_far],
-        [(1, NEAR_A), (1, NEAR_B), (0, FAR), (1, FAR)], state, everything, False,
-    )
+    own = closing(meta, order, q0, 0, late + last, late_blocks + last_blocks, state, everything, False)
     return join(own, came)
 
 

time: 73.1 us -> 80.7 us (1.10)
  the two profiles are of different devices: /device:TPU:32 before, /device:TPU:56 now
where the time goes in v3:
time: 80.7 us; the launch traced here: 79.2 us
  Pallas kernels  41.7 us (52%)
  starting transfers between devices  18.5 us (23%)
  waiting for transfers between devices  16.7 us (21%)
  local copies, waits for them, and re-layouts  2.1 us (3%)
    pallas_call x2, Pallas kernels, stage(): pl.pallas_call(kernel, out_shape=[jax.ShapeDtypeStruct((2,) + ACC, F32),...  19.9 us
    ppermute x15, starting transfers between devices, send(): return lax.ppermute(array, ('ctx', 'head'), perm)  18.5 us
    ppermute x15, waiting for transfers between devices, send(): return lax.ppermute(array, ('ctx', 'head'), perm)  16.7 us
    pallas_call x3, Pallas kernels, closing(): pl.pallas_call(kernel, out_shape=out_shape, in_specs=[SMEM, SMEM] + [VMEM...  16.1 us
    pallas_call x1, Pallas kernels, diagonal(): pl.pallas_call(diagonal_kernel, out_shape=[jax.ShapeDtypeStruct((QH, ROWS...  2.5 us
    unnamed x12, local copies, waits for them, and re-layouts  2.1 us
    pallas_call x1, Pallas kernels, packed_kv(): pl.pallas_call(pack_kernel, out_shape=[jax.ShapeDtypeStruct((rows, 2 * HD...  2.1 us
  transfers between devices with their start and end apart: 15, of which 3 were waited for; matrix products, arithmetic and copies ran while one was open for 0% of the time, Pallas kernels for 45%

profile of v3, /device:TPU:56, one launch (start us, length us, event | category | flops | bytes accessed | tf_op | source)
XLA Modules:
  0.0 79.2 jit_solution(17151719847525638315)
XLA Ops:
  0.0 2.1 %pack_kv.1 = (bf16[1024,256]{1,0:T(8,128)(2,1)}, bf16[512,256]{1,0:T(8,128)(2,1)}, bf16[512,256]{1,0:T(8,128)(2,1)}) custom-call(bf16[1024,128]{1,0:T(8,128)(2,1)} %keys.1, bf16[1024,128]{1,0:T(8,128)(2,1)} %values.1), custom_call_target="tpu_custom_call" | custom-call | tf_op jit(solution)/shard_map/pack_kv/pallas_call | solution.py:338
  2.1 0.7 collective-permute-start.3
  2.8 1.1 %collective-permute-start.2 = (bf16[1024,256]{1,0:T(8,128)(2,1)}, bf16[1024,256]{1,0:T(8,128)(2,1)S(1)}, u32[]{:S(2)}, u32[]{:S(2)}) collective-permute-start(bf16[1024,256]{1,0:T(8,128)(2,1)} %refs_2_.1), channel_id=1, source_target_pairs={{0,192},{1,65},{2,194},{3,67},{4,196},{5,69},{6,198},{7,71},{8,200... | collective-permute-start | bytes 1572872 | tf_op jit(solution)/shard_map/ppermute | solution.py:52
  3.9 3.3 %collective-permute-start.4 = (bf16[512,256]{1,0:T(8,128)(2,1)}, bf16[512,256]{1,0:T(8,128)(2,1)S(1)}, u32[]{:S(2)}, u32[]{:S(2)}) collective-permute-start(bf16[512,256]{1,0:T(8,128)(2,1)} %get-tuple-element.26), channel_id=1, source_target_pairs={{0,16},{1,49},{2,18},{3,51},{4,20},{5,53},{6,22},{7,55},{8,24},{9,... | collective-permute-start | bytes 786440 | tf_op jit(solution)/shard_map/ppermute | solution.py:52
  7.2 2.1 %collective-permute-start.5 = (bf16[512,256]{1,0:T(8,128)(2,1)}, bf16[512,256]{1,0:T(8,128)(2,1)S(1)}, u32[]{:S(2)}, u32[]{:S(2)}) collective-permute-start(bf16[512,256]{1,0:T(8,128)(2,1)} %get-tuple-element.26), channel_id=1, source_target_pairs={{0,48},{1,17},{2,50},{3,19},{4,52},{5,21},{6,54},{7,23},{8,56},{9,... | collective-permute-start | bytes 786440 | tf_op jit(solution)/shard_map/ppermute | solution.py:52
  9.3 1.5 %collective-permute-start = (bf16[512,256]{1,0:T(8,128)(2,1)}, bf16[512,256]{1,0:T(8,128)(2,1)S(1)}, u32[]{:S(2)}, u32[]{:S(2)}) collective-permute-start(bf16[512,256]{1,0:T(8,128)(2,1)} %get-tuple-element.24), channel_id=1, source_target_pairs={{0,16},{1,49},{2,18},{3,51},{4,20},{5,53},{6,22},{7,55},{8,24},{9,... | collective-permute-start | bytes 786440 | tf_op jit(solution)/shard_map/ppermute | solution.py:52
  10.8 1.0 %copy-done = bf16[1024,256]{1,0:T(8,128)(2,1)S(1)} copy-done((bf16[1024,256]{1,0:T(8,128)(2,1)S(1)}, bf16[1024,256]{1,0:T(8,128)(2,1)}, u32[]{:S(2)}) %copy-start) | copy-done | bytes 524312
  11.9 1.0 %copy-done.2 = bf16[1024,256]{1,0:T(8,128)(2,1)S(1)} copy-done((bf16[1024,256]{1,0:T(8,128)(2,1)S(1)}, bf16[1024,256]{1,0:T(8,128)(2,1)}, u32[]{:S(2)}) %copy-start.2) | copy-done | bytes 524312
  12.9 2.5 %diagonal.1 = (f32[2,136,1024]{2,1,0:T(8,128)S(1)}, f32[2,1,1024]{2,1,0:T(1,128)S(1)}) custom-call(bf16[1024,256]{1,0:T(8,128)(2,1)S(1)} %copy-done, bf16[1024,256]{1,0:T(8,128)(2,1)S(1)} %copy-done.2), custom_call_target="tpu_custom_call" | custom-call | flops 3221225472 | bytes 4194304 | tf_op jit(solution)/shard_map/diagonal/pallas_call | solution.py:97
  15.4 11.7 %collective-permute-done.4.refs_6_.refs_12_.refs_8_ = bf16[512,256]{1,0:T(8,128)(2,1)S(1)} collective-permute-done((bf16[512,256]{1,0:T(8,128)(2,1)}, bf16[512,256]{1,0:T(8,128)(2,1)S(1)}, u32[]{:S(2)}, u32[]{:S(2)}) %collective-permute-start.4) | collective-permute-done | bytes 262176 | tf_op jit(solution)/shard_map/ppermute | solution.py:52
  27.2 3.2 %collective-permute-start.1 = (bf16[512,256]{1,0:T(8,128)(2,1)S(1)}, bf16[512,256]{1,0:T(8,128)(2,1)S(1)}, u32[]{:S(2)}, u32[]{:S(2)}) collective-permute-start(bf16[512,256]{1,0:T(8,128)(2,1)S(1)} %copy-done.5), channel_id=1, source_target_pairs={{0,48},{1,17},{2,50},{3,19},{4,52},{5,21},{6,54},{7,23},{8,56},{9,... | collective-permute-start | bytes 786440 | tf_op jit(solution)/shard_map/ppermute | solution.py:52
  30.5 2.0 %collective-permute-start.11 = (bf16[512,256]{1,0:T(8,128)(2,1)S(1)}, bf16[512,256]{1,0:T(8,128)(2,1)S(1)}, u32[]{:S(2)}, u32[]{:S(2)}) collective-permute-start(bf16[512,256]{1,0:T(8,128)(2,1)S(1)} %collective-permute-done.5.refs_7_.refs_14_.refs_10_), channel_id=1, source_target_pairs={{0,64},{1,193},{2,66},{3,195},{4,68},{5,197},{6,70},{7,199},{8,72}... | collective-permute-start | bytes 786440 | tf_op jit(solution)/shard_map/ppermute | solution.py:52
  32.5 11.3 %stage.2 = (f32[2,2,136,1024]{3,2,1,0:T(8,128)S(1)}, f32[2,2,1,1024]{3,2,1,0:T(1,128)S(1)}) custom-call(s32[4]{0:T(128)S(1)} %pad_add_fusion.refs_0_, s32[16]{0:T(128)S(1)} %copy-done.4, bf16[1024,256]{1,0:T(8,128)(2,1)S(1)} %collective-permute-done.2.refs_2_, bf16[1024,256]{1,0:T(8,128)(2,1)S(1)} %copy-done, bf16[1024,256]{1,0:T(8,128)(2,1)S(1)} %copy-done.2, ...), custom_call_target="tpu_custom_call" | custom-call | flops 12884901888 | bytes 8388608 | tf_op jit(solution)/shard_map/stage/pallas_call | solution.py:187
  43.9 0.1 collective-permute-start.6
  44.0 2.0 %collective-permute-start.7 = (bf16[512,256]{1,0:T(8,128)(2,1)S(1)}, bf16[512,256]{1,0:T(8,128)(2,1)S(1)}, u32[]{:S(2)}, u32[]{:S(2)}) collective-permute-start(bf16[512,256]{1,0:T(8,128)(2,1)S(1)} %collective-permute-done.1.refs_5_.refs_15_.refs_11_), channel_id=1, source_target_pairs={{0,64},{1,193},{2,66},{3,195},{4,68},{5,197},{6,70},{7,199},{8,72}... | collective-permute-start | bytes 786440 | tf_op jit(solution)/shard_map/ppermute | solution.py:52
  46.0 8.6 %stage.3 = (f32[2,2,136,1024]{3,2,1,0:T(8,128)S(1)}, f32[2,2,1,1024]{3,2,1,0:T(1,128)S(1)}) custom-call(s32[4]{0:T(128)S(1)} %pad_add_fusion.refs_0_, s32[16]{0:T(128)S(1)} %copy-done.4, bf16[1024,256]{1,0:T(8,128)(2,1)S(1)} %collective-permute-done.2.refs_2_, bf16[1024,256]{1,0:T(8,128)(2,1)S(1)} %copy-done.1, ...), custom_call_target="tpu_custom_call" | custom-call | flops 8589934592 | bytes 8388608 | tf_op jit(solution)/shard_map/stage/pallas_call | solution.py:187
  54.7 2.0 %collective-permute-start.13 = (bf16[512,256]{1,0:T(8,128)(2,1)S(1)}, bf16[512,256]{1,0:T(8,128)(2,1)S(1)}, u32[]{:S(2)}, u32[]{:S(2)}) collective-permute-start(bf16[512,256]{1,0:T(8,128)(2,1)S(1)} %collective-permute-done.9.refs_6_.refs_17_.refs_13_), channel_id=1, source_target_pairs={{0,64},{1,193},{2,66},{3,195},{4,68},{5,197},{6,70},{7,199},{8,72}... | collective-permute-start | bytes 786440 | tf_op jit(solution)/shard_map/ppermute | solution.py:52
  56.7 5.2 %guest.1 = (f32[1,2,136,1024]{3,2,1,0:T(8,128)S(1)}, f32[1,2,1,1024]{3,2,1,0:T(1,128)S(1)}) custom-call(s32[4]{0:T(128)S(1)} %pad_add_fusion.refs_0_, s32[16]{0:T(128)S(1)} %copy-done.4, bf16[1024,256]{1,0:T(8,128)(2,1)S(1)} %collective-permute-done.2.refs_2_, bf16[512,256]{1,0:T(8,128)(2,1)S(1)} %collective-permute-done.6.refs_3_.refs_20_.refs_16_, ...), custom_call_target="tpu_custom_call" | custom-call | flops 4294967296 | bytes 8388608 | tf_op jit(solution)/shard_map/guest/pallas_call | solution.py:287
  62.0 1.9 %collective-permute-done.13.refs_8_.refs_24_.refs_4_.refs_20_ = bf16[512,256]{1,0:T(8,128)(2,1)S(1)} collective-permute-done((bf16[512,256]{1,0:T(8,128)(2,1)S(1)}, bf16[512,256]{1,0:T(8,128)(2,1)S(1)}, u32[]{:S(2)}, u32[]{:S(2)}) %collective-permute-start.13) | collective-permute-done | bytes 262176 | tf_op jit(solution)/shard_map/ppermute | solution.py:52
  63.9 3.2 %away.1 = bf16[272,1024]{1,0:T(8,128)(2,1)S(1)} custom-call(s32[4]{0:T(128)S(1)} %pad_add_fusion.refs_0_, s32[16]{0:T(128)S(1)} %copy-done.4, bf16[1024,256]{1,0:T(8,128)(2,1)S(1)} %collective-permute-done.2.refs_2_, bf16[512,256]{1,0:T(8,128)(2,1)S(1)} %collective-permute-done.12.refs_7_.refs_23_.refs_3_.refs_19_, ...), custom_call_target="tpu_custom_call" | custom-call | flops 2147483648 | bytes 8388608 | tf_op jit(solution)/shard_map/away/pallas_call | solution.py:287
  67.1 0.3 collective-permute-start.14
  67.4 7.7 %home.1 = (f32[1,2,136,1024]{3,2,1,0:T(8,128)S(1)}, f32[1,2,1,1024]{3,2,1,0:T(1,128)S(1)}) custom-call(s32[4]{0:T(128)S(1)} %pad_add_fusion.refs_0_, s32[16]{0:T(128)S(1)} %copy-done.4, bf16[1024,256]{1,0:T(8,128)(2,1)S(1)} %copy-done.1, bf16[512,256]{1,0:T(8,128)(2,1)S(1)} %collective-permute-done.6.refs_3_.refs_20_.refs_16_, ...), custom_call_target="tpu_custom_call" | custom-call | flops 6442450944 | bytes 8388608 | tf_op jit(solution)/shard_map/home/pallas_call | solution.py:287
  75.1 3.0 %collective-permute-done.14.came = bf16[272,1024]{1,0:T(8,128)(2,1)S(1)} collective-permute-done((bf16[272,1024]{1,0:T(8,128)(2,1)S(1)}, bf16[272,1024]{1,0:T(8,128)(2,1)S(1)}, u32[]{:S(2)}, u32[]{:S(2)}) %collective-permute-start.14) | collective-permute-done | bytes 557088 | tf_op jit(solution)/shard_map/ppermute | solution.py:52
  78.1 1.1 %join.1 = bf16[1024,256]{1,0:T(8,128)(2,1)} custom-call(f32[1,2,136,1024]{3,2,1,0:T(8,128)S(1)} %get-tuple-element.39.acc, f32[1,2,1,1024]{3,2,1,0:T(1,128)S(1)} %get-tuple-element.40.shift, bf16[272,1024]{1,0:T(8,128)(2,1)S(1)} %collective-permute-done.14.came), custom_call_target="tpu_custom_call" | custom-call | tf_op jit(solution)/shard_map/join/pallas_call | solution.py:316
  (27 shorter events, 0.4 us)
Async XLA Ops:
  2.1 28.3 %collective-permute-start.3 = (bf16[1024,256]{1,0:T(8,128)(2,1)}, bf16[1024,256]{1,0:T(8,128)(2,1)S(1)}, u32[]{:S(2)}, u32[]{:S(2)}) collective-permute-start(bf16[1024,256]{1,0:T(8,128)(2,1)} %get-tuple-element.25.kv_ref.refs_4_.refs_11_.refs_7_), channel_id=1, source_target_pairs={{0,64},{1,193},{2,66},{3,195},{4,68},{5,197},{6,70},{7,199},{8,72}... | collective-permute-start | bytes 1572872 | tf_op jit(solution)/shard_map/ppermute | solution.py:52
  2.8 27.6 %collective-permute-start.2 = (bf16[1024,256]{1,0:T(8,128)(2,1)}, bf16[1024,256]{1,0:T(8,128)(2,1)S(1)}, u32[]{:S(2)}, u32[]{:S(2)}) collective-permute-start(bf16[1024,256]{1,0:T(8,128)(2,1)} %refs_2_.1), channel_id=1, source_target_pairs={{0,192},{1,65},{2,194},{3,67},{4,196},{5,69},{6,198},{7,71},{8,200... | collective-permute-start | bytes 1572872 | tf_op jit(solution)/shard_map/ppermute | solution.py:52
  3.9 23.3 %collective-permute-start.4 = (bf16[512,256]{1,0:T(8,128)(2,1)}, bf16[512,256]{1,0:T(8,128)(2,1)S(1)}, u32[]{:S(2)}, u32[]{:S(2)}) collective-permute-start(bf16[512,256]{1,0:T(8,128)(2,1)} %get-tuple-element.26), channel_id=1, source_target_pairs={{0,16},{1,49},{2,18},{3,51},{4,20},{5,53},{6,22},{7,55},{8,24},{9,... | collective-permute-start | bytes 786440 | tf_op jit(solution)/shard_map/ppermute | solution.py:52
  7.2 23.2 %collective-permute-start.5 = (bf16[512,256]{1,0:T(8,128)(2,1)}, bf16[512,256]{1,0:T(8,128)(2,1)S(1)}, u32[]{:S(2)}, u32[]{:S(2)}) collective-permute-start(bf16[512,256]{1,0:T(8,128)(2,1)} %get-tuple-element.26), channel_id=1, source_target_pairs={{0,48},{1,17},{2,50},{3,19},{4,52},{5,21},{6,54},{7,23},{8,56},{9,... | collective-permute-start | bytes 786440 | tf_op jit(solution)/shard_map/ppermute | solution.py:52
  9.3 34.4 %collective-permute-start = (bf16[512,256]{1,0:T(8,128)(2,1)}, bf16[512,256]{1,0:T(8,128)(2,1)S(1)}, u32[]{:S(2)}, u32[]{:S(2)}) collective-permute-start(bf16[512,256]{1,0:T(8,128)(2,1)} %get-tuple-element.24), channel_id=1, source_target_pairs={{0,16},{1,49},{2,18},{3,51},{4,20},{5,53},{6,22},{7,55},{8,24},{9,... | collective-permute-start | bytes 786440 | tf_op jit(solution)/shard_map/ppermute | solution.py:52
  10.8 1.0 %copy-start = (bf16[1024,256]{1,0:T(8,128)(2,1)S(1)}, bf16[1024,256]{1,0:T(8,128)(2,1)}, u32[]{:S(2)}) copy-start(bf16[1024,256]{1,0:T(8,128)(2,1)} %refs_2_.1) | copy-start | bytes 1572868
  11.9 1.0 %copy-start.2 = (bf16[1024,256]{1,0:T(8,128)(2,1)S(1)}, bf16[1024,256]{1,0:T(8,128)(2,1)}, u32[]{:S(2)}) copy-start(bf16[1024,256]{1,0:T(8,128)(2,1)} %get-tuple-element.25.kv_ref.refs_4_.refs_11_.refs_7_) | copy-start | bytes 1572868
  12.9 14.3 %copy-start.5 = (bf16[512,256]{1,0:T(8,128)(2,1)S(1)}, bf16[512,256]{1,0:T(8,128)(2,1)}, u32[]{:S(2)}) copy-start(bf16[512,256]{1,0:T(8,128)(2,1)} %get-tuple-element.24) | copy-start | bytes 786436
  12.9 19.6 %copy-start.4 = (s32[16]{0:T(128)S(1)}, s32[16]{0:T(128)}, u32[]{:S(2)}) copy-start(s32[16]{0:T(128)} %refs_1_.9) | copy-start | bytes 196
  27.2 16.6 %collective-permute-start.1 = (bf16[512,256]{1,0:T(8,128)(2,1)S(1)}, bf16[512,256]{1,0:T(8,128)(2,1)S(1)}, u32[]{:S(2)}, u32[]{:S(2)}) collective-permute-start(bf16[512,256]{1,0:T(8,128)(2,1)S(1)} %copy-done.5), channel_id=1, source_target_pairs={{0,48},{1,17},{2,50},{3,19},{4,52},{5,21},{6,54},{7,23},{8,56},{9,... | collective-permute-start | bytes 786440 | tf_op jit(solution)/shard_map/ppermute | solution.py:52
  30.4 13.6 %collective-permute-start.10 = (bf16[512,256]{1,0:T(8,128)(2,1)S(1)}, bf16[512,256]{1,0:T(8,128)(2,1)S(1)}, u32[]{:S(2)}, u32[]{:S(2)}) collective-permute-start(bf16[512,256]{1,0:T(8,128)(2,1)S(1)} %collective-permute-done.4.refs_6_.refs_12_.refs_8_), channel_id=1, source_target_pairs={{0,64},{1,193},{2,66},{3,195},{4,68},{5,197},{6,70},{7,199},{8,72}... | collective-permute-start | bytes 786440 | tf_op jit(solution)/shard_map/ppermute | solution.py:52
  30.4 24.2 %collective-permute-start.8 = (bf16[512,256]{1,0:T(8,128)(2,1)S(1)}, bf16[512,256]{1,0:T(8,128)(2,1)S(1)}, u32[]{:S(2)}, u32[]{:S(2)}) collective-permute-start(bf16[512,256]{1,0:T(8,128)(2,1)S(1)} %collective-permute-done.4.refs_6_.refs_12_.refs_8_), channel_id=1, source_target_pairs={{0,16},{1,49},{2,18},{3,51},{4,20},{5,53},{6,22},{7,55},{8,24},{9,... | collective-permute-start | bytes 786440 | tf_op jit(solution)/shard_map/ppermute | solution.py:52
  30.5 15.5 %collective-permute-start.11 = (bf16[512,256]{1,0:T(8,128)(2,1)S(1)}, bf16[512,256]{1,0:T(8,128)(2,1)S(1)}, u32[]{:S(2)}, u32[]{:S(2)}) collective-permute-start(bf16[512,256]{1,0:T(8,128)(2,1)S(1)} %collective-permute-done.5.refs_7_.refs_14_.refs_10_), channel_id=1, source_target_pairs={{0,64},{1,193},{2,66},{3,195},{4,68},{5,197},{6,70},{7,199},{8,72}... | collective-permute-start | bytes 786440 | tf_op jit(solution)/shard_map/ppermute | solution.py:52
  32.5 13.5 %copy-start.1 = (bf16[1024,256]{1,0:T(8,128)(2,1)S(1)}, bf16[1024,256]{1,0:T(8,128)(2,1)}, u32[]{:S(2)}) copy-start(bf16[1024,256]{1,0:T(8,128)(2,1)} %refs_2_.1) | copy-start | bytes 1572868
  43.8 10.8 %collective-permute-start.9 = (bf16[512,256]{1,0:T(8,128)(2,1)S(1)}, bf16[512,256]{1,0:T(8,128)(2,1)S(1)}, u32[]{:S(2)}, u32[]{:S(2)}) collective-permute-start(bf16[512,256]{1,0:T(8,128)(2,1)S(1)} %collective-permute-done.refs_4_.refs_13_.refs_9_), channel_id=1, source_target_pairs={{0,16},{1,49},{2,18},{3,51},{4,20},{5,53},{6,22},{7,55},{8,24},{9,... | collective-permute-start | bytes 786440 | tf_op jit(solution)/shard_map/ppermute | solution.py:52
  43.9 12.9 %collective-permute-start.6 = (bf16[512,256]{1,0:T(8,128)(2,1)S(1)}, bf16[512,256]{1,0:T(8,128)(2,1)S(1)}, u32[]{:S(2)}, u32[]{:S(2)}) collective-permute-start(bf16[512,256]{1,0:T(8,128)(2,1)S(1)} %collective-permute-done.refs_4_.refs_13_.refs_9_), channel_id=1, source_target_pairs={{0,64},{1,193},{2,66},{3,195},{4,68},{5,197},{6,70},{7,199},{8,72}... | collective-permute-start | bytes 786440 | tf_op jit(solution)/shard_map/ppermute | solution.py:52
  44.0 12.8 %collective-permute-start.7 = (bf16[512,256]{1,0:T(8,128)(2,1)S(1)}, bf16[512,256]{1,0:T(8,128)(2,1)S(1)}, u32[]{:S(2)}, u32[]{:S(2)}) collective-permute-start(bf16[512,256]{1,0:T(8,128)(2,1)S(1)} %collective-permute-done.1.refs_5_.refs_15_.refs_11_), channel_id=1, source_target_pairs={{0,64},{1,193},{2,66},{3,195},{4,68},{5,197},{6,70},{7,199},{8,72}... | collective-permute-start | bytes 786440 | tf_op jit(solution)/shard_map/ppermute | solution.py:52
  54.6 7.3 %collective-permute-start.12 = (bf16[512,256]{1,0:T(8,128)(2,1)S(1)}, bf16[512,256]{1,0:T(8,128)(2,1)S(1)}, u32[]{:S(2)}, u32[]{:S(2)}) collective-permute-start(bf16[512,256]{1,0:T(8,128)(2,1)S(1)} %collective-permute-done.8.refs_5_.refs_16_.refs_12_), channel_id=1, source_target_pairs={{0,64},{1,193},{2,66},{3,195},{4,68},{5,197},{6,70},{7,199},{8,72}... | collective-permute-start | bytes 786440 | tf_op jit(solution)/shard_map/ppermute | solution.py:52
  54.7 9.2 %collective-permute-start.13 = (bf16[512,256]{1,0:T(8,128)(2,1)S(1)}, bf16[512,256]{1,0:T(8,128)(2,1)S(1)}, u32[]{:S(2)}, u32[]{:S(2)}) collective-permute-start(bf16[512,256]{1,0:T(8,128)(2,1)S(1)} %collective-permute-done.9.refs_6_.refs_17_.refs_13_), channel_id=1, source_target_pairs={{0,64},{1,193},{2,66},{3,195},{4,68},{5,197},{6,70},{7,199},{8,72}... | collective-permute-start | bytes 786440 | tf_op jit(solution)/shard_map/ppermute | solution.py:52
  56.7 7.2 %copy-start.3 = (bf16[1024,256]{1,0:T(8,128)(2,1)S(1)}, bf16[1024,256]{1,0:T(8,128)(2,1)}, u32[]{:S(2)}) copy-start(bf16[1024,256]{1,0:T(8,128)(2,1)} %get-tuple-element.25.kv_ref.refs_4_.refs_11_.refs_7_) | copy-start | bytes 1572868
  67.1 11.1 %collective-permute-start.14 = (bf16[272,1024]{1,0:T(8,128)(2,1)S(1)}, bf16[272,1024]{1,0:T(8,128)(2,1)S(1)}, u32[]{:S(2)}, u32[]{:S(2)}) collective-permute-start(bf16[272,1024]{1,0:T(8,128)(2,1)S(1)} %away.1), channel_id=1, source_target_pairs={{0,192},{1,65},{2,194},{3,67},{4,196},{5,69},{6,198},{7,71},{8,200... | collective-permute-start | bytes 1671176 | tf_op jit(solution)/shard_map/ppermute | solution.py:52

commit v4 on v2

--- a/solution.py
+++ b/solution.py
@@ -42,7 +42,7 @@
 
 def ring_perm(sign):
     return [
-        ((y * 4 + z) * 16 + h, (y * 4 + (z + (sign if h % 2 == 0 else -sign)) % 4) * 16 + h)
+        ((y * 4 + z) * 16 + h, (y * 4 + (z + (sign if h // 2 % 2 == 0 else -sign)) % 4) * 16 + h)
         for y in range(4) for z in range(4) for h in range(16)
     ]
 
@@ -332,42 +332,47 @@
 
 def body(q0, keys, values, order):
     index = lax.axis_index("ctx")
-    core = lax.axis_index("head") & 1
+    place = lax.axis_index("head")
+    core, low = place & 1, place >> 1 & 1
     y, z = index >> 2, index & 3
     even, odd = y ^ 1, (((y + 3) & 3 ^ 1) + 1) & 3
     key_y = jnp.where(core == 0, even, odd)
     query_y = jnp.where(core == 0, odd, even)
-    meta = jnp.stack([index, key_y * 4 + z, query_y * 4 + z, jnp.where(core == 0, 3, 1)]).astype(jnp.int32)
+    meta = jnp.stack([index, key_y * 4 + z, query_y * 4 + z, jnp.where(low == 0, 3, 1)]).astype(jnp.int32)
 
     key_perm, query_perm = mate_perm(key_mate), mate_perm(query_mate)
     forth, back = ring_perm(1), ring_perm(-1)
     kv = packed_kv(keys, values)
     near_a = send(kv, forth)
-    near_b = send(kv, back)
-    acc, shift = diagonal(q0, kv)
     mate_own = send(kv, key_perm)
     q1 = send(q0, query_perm)
+    state0 = diagonal(q0, kv)
+
+    kv, near_a = lax.optimization_barrier((kv, near_a))
+    near_b = send(kv, back)
+    mate_a = send(near_a, key_perm)
     qs = [q1, q0]
-    state = stage(meta, order, qs, [kv, mate_own], [(0, OWN), (1, OWN)], [None, (acc, shift)])
+    state = stage(
+        meta, order, qs, [kv, mate_own, near_a], [(0, OWN), (1, OWN), (0, NEAR_A)], [None, state0]
+    )
 
     near_a, near_b, shift = lax.optimization_barrier((near_a, near_b, state[1]))
     far = send(near_a, forth)
-    mate_a = send(near_a, key_perm)
     mate_b = send(near_b, key_perm)
-    state = stage(meta, order, qs, [near_a, near_b], [(0, NEAR_A), (0, NEAR_B)], [state[0], shift])
+    state = stage(meta, order, qs, [mate_a, near_b], [(1, NEAR_A), (0, NEAR_B)], [state[0], shift])
 
     far, shift = lax.optimization_barrier((far, state[1]))
     state = [state[0], shift]
     mate_far = send(far, key_perm)
     guest = closing(
-        meta, order, q1, 2, [mate_a, mate_b, far], [(1, NEAR_A), (1, NEAR_B), (0, FAR)], state, [], False
+        meta, order, q1, 2, [mate_b, far], [(1, NEAR_B), (0, FAR)], state, [], False
     )
     everything = [kv, near_a, near_b, far, mate_own, mate_a, mate_b, mate_far]
     away = closing(meta, order, q1, 2, [mate_far], [(1, FAR)], guest, everything, True)
     came = send(away, query_perm)
     own = closing(
-        meta, order, q0, 0, [mate_a, mate_b, far, mate_far],
-        [(1, NEAR_A), (1, NEAR_B), (0, FAR), (1, FAR)], state, everything, False,
+        meta, order, q0, 0, [mate_b, far, mate_far],
+        [(1, NEAR_B), (0, FAR), (1, FAR)], state, everything, False,
     )
     return join(own, came)
 

time: 73.1 us -> 73.2 us (level)
  the two profiles are of different devices: /device:TPU:32 before, /device:TPU:6 now
where the time goes in v4:
time: 73.2 us; the launch traced here: 74.1 us
  Pallas kernels  41.6 us (57%)
  starting transfers between devices  18.8 us (26%)
  waiting for transfers between devices  12.5 us (17%)
  local copies, waits for them, and re-layouts  1.05 us (1%)
    pallas_call x2, Pallas kernels, stage(): pl.pallas_call(kernel, out_shape=[jax.ShapeDtypeStruct((2,) + ACC, F32),...  20.2 us
    ppermute x9, starting transfers between devices, send(): return lax.ppermute(array, ('ctx', 'head'), perm)  18.8 us
    pallas_call x3, Pallas kernels, closing(): pl.pallas_call(kernel, out_shape=out_shape, in_specs=[SMEM, SMEM] + [VMEM...  14.7 us
    ppermute x9, waiting for transfers between devices, send(): return lax.ppermute(array, ('ctx', 'head'), perm)  12.5 us
    pallas_call x1, Pallas kernels, diagonal(): pl.pallas_call(diagonal_kernel, out_shape=[jax.ShapeDtypeStruct((QH, ROWS...  3.61 us
    pallas_call x1, Pallas kernels, packed_kv(): pl.pallas_call(pack_kernel, out_shape=jax.ShapeDtypeStruct((TOK, 2 * HD),...  1.94 us
  transfers between devices with their start and end apart: 9, of which 4 were waited for; matrix products, arithmetic and copies ran while one was open for 0% of the time, Pallas kernels for 48%

profile of v4, /device:TPU:6, one launch (start us, length us, event | category | flops | bytes accessed | tf_op | source)
XLA Modules:
  0.0 74.1 jit_solution(12030032733302985905)
XLA Ops:
  0.0 1.9 %pack_kv.1.kv_ref.refs_4_.refs_8_.refs_6_ = bf16[1024,256]{1,0:T(8,128)(2,1)} custom-call(bf16[1024,128]{1,0:T(8,128)(2,1)} %keys.1, bf16[1024,128]{1,0:T(8,128)(2,1)} %values.1), custom_call_target="tpu_custom_call" | custom-call | tf_op jit(solution)/shard_map/pack_kv/pallas_call | solution.py:324
  1.9 3.3 %collective-permute-start = (bf16[1024,256]{1,0:T(8,128)(2,1)}, bf16[1024,256]{1,0:T(8,128)(2,1)S(1)}, u32[]{:S(2)}, u32[]{:S(2)}) collective-permute-start(bf16[1024,256]{1,0:T(8,128)(2,1)} %pack_kv.1.kv_ref.refs_4_.refs_8_.refs_6_), channel_id=1, source_target_pairs={{0,16},{1,17},{2,50},{3,51},{4,20},{5,21},{6,54},{7,55},{8,24},{9,... | collective-permute-start | bytes 1572872 | tf_op jit(solution)/shard_map/ppermute | solution.py:51
  5.2 1.6 %collective-permute-start.3 = (bf16[1024,256]{1,0:T(8,128)(2,1)}, bf16[1024,256]{1,0:T(8,128)(2,1)S(1)}, u32[]{:S(2)}, u32[]{:S(2)}) collective-permute-start(bf16[1024,256]{1,0:T(8,128)(2,1)} %pack_kv.1.kv_ref.refs_4_.refs_8_.refs_6_), channel_id=1, source_target_pairs={{0,64},{1,193},{2,66},{3,195},{4,68},{5,197},{6,70},{7,199},{8,72}... | collective-permute-start | bytes 1572872 | tf_op jit(solution)/shard_map/ppermute | solution.py:51
  6.8 2.2 %collective-permute-start.2 = (bf16[1024,256]{1,0:T(8,128)(2,1)}, bf16[1024,256]{1,0:T(8,128)(2,1)S(1)}, u32[]{:S(2)}, u32[]{:S(2)}) collective-permute-start(bf16[1024,256]{1,0:T(8,128)(2,1)} %refs_2_.1), channel_id=1, source_target_pairs={{0,192},{1,65},{2,194},{3,67},{4,196},{5,69},{6,198},{7,71},{8,200... | collective-permute-start | bytes 1572872 | tf_op jit(solution)/shard_map/ppermute | solution.py:51
  9.0 0.1 pad_add_fusion.refs_0_
  9.1 1.0 %copy-done = bf16[1024,256]{1,0:T(8,128)(2,1)S(1)} copy-done((bf16[1024,256]{1,0:T(8,128)(2,1)S(1)}, bf16[1024,256]{1,0:T(8,128)(2,1)}, u32[]{:S(2)}) %copy-start) | copy-done | bytes 524312
  10.1 3.6 %diagonal.1 = (f32[2,136,1024]{2,1,0:T(8,128)S(1)}, f32[2,1,1024]{2,1,0:T(1,128)S(1)}) custom-call(bf16[1024,256]{1,0:T(8,128)(2,1)S(1)} %copy-done, bf16[1024,256]{1,0:T(8,128)(2,1)} %pack_kv.1.kv_ref.refs_4_.refs_8_.refs_6_), custom_call_target="tpu_custom_call" | custom-call | flops 3221225472 | bytes 4194304 | tf_op jit(solution)/shard_map/diagonal/pallas_call | solution.py:96
  13.7 6.7 %collective-permute-done.refs_6_.refs_9_.refs_7_ = bf16[1024,256]{1,0:T(8,128)(2,1)S(1)} collective-permute-done((bf16[1024,256]{1,0:T(8,128)(2,1)}, bf16[1024,256]{1,0:T(8,128)(2,1)S(1)}, u32[]{:S(2)}, u32[]{:S(2)}) %collective-permute-start) | collective-permute-done | bytes 524320 | tf_op jit(solution)/shard_map/ppermute | solution.py:51
  20.4 2.6 %collective-permute-start.1 = (bf16[1024,256]{1,0:T(8,128)(2,1)}, bf16[1024,256]{1,0:T(8,128)(2,1)S(1)}, u32[]{:S(2)}, u32[]{:S(2)}) collective-permute-start(bf16[1024,256]{1,0:T(8,128)(2,1)} %pack_kv.1.kv_ref.refs_4_.refs_8_.refs_6_), channel_id=1, source_target_pairs={{0,48},{1,49},{2,18},{3,19},{4,52},{5,53},{6,22},{7,23},{8,56},{9,... | collective-permute-start | bytes 1572872 | tf_op jit(solution)/shard_map/ppermute | solution.py:51
  23.0 1.6 %collective-permute-start.6 = (bf16[1024,256]{1,0:T(8,128)(2,1)S(1)}, bf16[1024,256]{1,0:T(8,128)(2,1)S(1)}, u32[]{:S(2)}, u32[]{:S(2)}) collective-permute-start(bf16[1024,256]{1,0:T(8,128)(2,1)S(1)} %collective-permute-done.refs_6_.refs_9_.refs_7_), channel_id=1, source_target_pairs={{0,64},{1,193},{2,66},{3,195},{4,68},{5,197},{6,70},{7,199},{8,72}... | collective-permute-start | bytes 1572872 | tf_op jit(solution)/shard_map/ppermute | solution.py:51
  24.6 0.0 collective-permute-done.3.refs_5_.refs_12_.refs_10_
  24.6 11.4 %stage.2 = (f32[2,2,136,1024]{3,2,1,0:T(8,128)S(1)}, f32[2,2,1,1024]{3,2,1,0:T(1,128)S(1)}) custom-call(s32[4]{0:T(128)S(1)} %pad_add_fusion.refs_0_, s32[16]{0:T(128)S(1)} %copy-done.2, bf16[1024,256]{1,0:T(8,128)(2,1)S(1)} %collective-permute-done.2.refs_2_, bf16[1024,256]{1,0:T(8,128)(2,1)S(1)} %copy-done.1, ...), custom_call_target="tpu_custom_call" | custom-call | flops 12884901888 | bytes 8388608 | tf_op jit(solution)/shard_map/stage/pallas_call | solution.py:177
  36.1 0.9 %collective-permute-start.5 = (bf16[1024,256]{1,0:T(8,128)(2,1)S(1)}, bf16[1024,256]{1,0:T(8,128)(2,1)S(1)}, u32[]{:S(2)}, u32[]{:S(2)}) collective-permute-start(bf16[1024,256]{1,0:T(8,128)(2,1)S(1)} %collective-permute-done.refs_6_.refs_9_.refs_7_), channel_id=1, source_target_pairs={{0,16},{1,17},{2,50},{3,51},{4,20},{5,21},{6,54},{7,55},{8,24},{9,... | collective-permute-start | bytes 1572872 | tf_op jit(solution)/shard_map/ppermute | solution.py:51
  36.9 1.6 %collective-permute-start.4 = (bf16[1024,256]{1,0:T(8,128)(2,1)S(1)}, bf16[1024,256]{1,0:T(8,128)(2,1)S(1)}, u32[]{:S(2)}, u32[]{:S(2)}) collective-permute-start(bf16[1024,256]{1,0:T(8,128)(2,1)S(1)} %collective-permute-done.1.refs_5_.refs_10_.refs_8_), channel_id=1, source_target_pairs={{0,64},{1,193},{2,66},{3,195},{4,68},{5,197},{6,70},{7,199},{8,72}... | collective-permute-start | bytes 1572872 | tf_op jit(solution)/shard_map/ppermute | solution.py:51
  38.5 8.7 %stage.3 = (f32[2,2,136,1024]{3,2,1,0:T(8,128)S(1)}, f32[2,2,1,1024]{3,2,1,0:T(1,128)S(1)}) custom-call(s32[4]{0:T(128)S(1)} %pad_add_fusion.refs_0_, s32[16]{0:T(128)S(1)} %copy-done.2, bf16[1024,256]{1,0:T(8,128)(2,1)S(1)} %collective-permute-done.2.refs_2_, bf16[1024,256]{1,0:T(8,128)(2,1)S(1)} %copy-done.1, ...), custom_call_target="tpu_custom_call" | custom-call | flops 8589934592 | bytes 8388608 | tf_op jit(solution)/shard_map/stage/pallas_call | solution.py:177
  47.3 1.6 %collective-permute-done.5.refs_4_.refs_11_.refs_9_ = bf16[1024,256]{1,0:T(8,128)(2,1)S(1)} collective-permute-done((bf16[1024,256]{1,0:T(8,128)(2,1)S(1)}, bf16[1024,256]{1,0:T(8,128)(2,1)S(1)}, u32[]{:S(2)}, u32[]{:S(2)}) %collective-permute-start.5) | collective-permute-done | bytes 524320 | tf_op jit(solution)/shard_map/ppermute | solution.py:51
  48.9 3.2 %collective-permute-start.7 = (bf16[1024,256]{1,0:T(8,128)(2,1)S(1)}, bf16[1024,256]{1,0:T(8,128)(2,1)S(1)}, u32[]{:S(2)}, u32[]{:S(2)}) collective-permute-start(bf16[1024,256]{1,0:T(8,128)(2,1)S(1)} %collective-permute-done.5.refs_4_.refs_11_.refs_9_), channel_id=1, source_target_pairs={{0,64},{1,193},{2,66},{3,195},{4,68},{5,197},{6,70},{7,199},{8,72}... | collective-permute-start | bytes 1572872 | tf_op jit(solution)/shard_map/ppermute | solution.py:51
  52.1 4.7 %guest.1 = (f32[1,2,136,1024]{3,2,1,0:T(8,128)S(1)}, f32[1,2,1,1024]{3,2,1,0:T(1,128)S(1)}) custom-call(s32[4]{0:T(128)S(1)} %pad_add_fusion.refs_0_, s32[16]{0:T(128)S(1)} %copy-done.2, bf16[1024,256]{1,0:T(8,128)(2,1)S(1)} %collective-permute-done.2.refs_2_, bf16[1024,256]{1,0:T(8,128)(2,1)S(1)} %collective-permute-done.4.refs_3_.refs_14_.refs_12_, ...), custom_call_target="tpu_custom_call" | custom-call | flops 4294967296 | bytes 8388608 | tf_op jit(solution)/shard_map/guest/pallas_call | solution.py:277
  56.8 2.5 %collective-permute-done.7.refs_5_.refs_15_.refs_3_.refs_13_ = bf16[1024,256]{1,0:T(8,128)(2,1)S(1)} collective-permute-done((bf16[1024,256]{1,0:T(8,128)(2,1)S(1)}, bf16[1024,256]{1,0:T(8,128)(2,1)S(1)}, u32[]{:S(2)}, u32[]{:S(2)}) %collective-permute-start.7) | collective-permute-done | bytes 524320 | tf_op jit(solution)/shard_map/ppermute | solution.py:51
  59.2 2.9 %away.1 = bf16[272,1024]{1,0:T(8,128)(2,1)S(1)} custom-call(s32[4]{0:T(128)S(1)} %pad_add_fusion.refs_0_, s32[16]{0:T(128)S(1)} %copy-done.2, bf16[1024,256]{1,0:T(8,128)(2,1)S(1)} %collective-permute-done.2.refs_2_, bf16[1024,256]{1,0:T(8,128)(2,1)S(1)} %collective-permute-done.7.refs_5_.refs_15_.refs_3_.refs_13_, ...), custom_call_target="tpu_custom_call" | custom-call | flops 2147483648 | bytes 8388608 | tf_op jit(solution)/shard_map/away/pallas_call | solution.py:277
  62.2 1.9 %collective-permute-start.8 = (bf16[272,1024]{1,0:T(8,128)(2,1)S(1)}, bf16[272,1024]{1,0:T(8,128)(2,1)S(1)}, u32[]{:S(2)}, u32[]{:S(2)}) collective-permute-start(bf16[272,1024]{1,0:T(8,128)(2,1)S(1)} %away.1), channel_id=1, source_target_pairs={{0,192},{1,65},{2,194},{3,67},{4,196},{5,69},{6,198},{7,71},{8,200... | collective-permute-start | bytes 1671176 | tf_op jit(solution)/shard_map/ppermute | solution.py:51
  64.1 7.1 %home.1 = (f32[1,2,136,1024]{3,2,1,0:T(8,128)S(1)}, f32[1,2,1,1024]{3,2,1,0:T(1,128)S(1)}) custom-call(s32[4]{0:T(128)S(1)} %pad_add_fusion.refs_0_, s32[16]{0:T(128)S(1)} %copy-done.2, bf16[1024,256]{1,0:T(8,128)(2,1)S(1)} %copy-done.1, bf16[1024,256]{1,0:T(8,128)(2,1)S(1)} %collective-permute-done.4.refs_3_.refs_14_.refs_12_, ...), custom_call_target="tpu_custom_call" | custom-call | flops 6442450944 | bytes 8388608 | tf_op jit(solution)/shard_map/home/pallas_call | solution.py:277
  71.2 1.8 %collective-permute-done.8.came = bf16[272,1024]{1,0:T(8,128)(2,1)S(1)} collective-permute-done((bf16[272,1024]{1,0:T(8,128)(2,1)S(1)}, bf16[272,1024]{1,0:T(8,128)(2,1)S(1)}, u32[]{:S(2)}, u32[]{:S(2)}) %collective-permute-start.8) | collective-permute-done | bytes 557088 | tf_op jit(solution)/shard_map/ppermute | solution.py:51
  73.0 1.1 %join.1 = bf16[1024,256]{1,0:T(8,128)(2,1)} custom-call(f32[1,2,136,1024]{3,2,1,0:T(8,128)S(1)} %get-tuple-element.35.acc, f32[1,2,1,1024]{3,2,1,0:T(1,128)S(1)} %get-tuple-element.36.shift, bf16[272,1024]{1,0:T(8,128)(2,1)S(1)} %collective-permute-done.8.came), custom_call_target="tpu_custom_call" | custom-call | tf_op jit(solution)/shard_map/join/pallas_call | solution.py:306
  (9 shorter events, 0.0 us)
Async XLA Ops:
  1.9 18.4 %collective-permute-start = (bf16[1024,256]{1,0:T(8,128)(2,1)}, bf16[1024,256]{1,0:T(8,128)(2,1)S(1)}, u32[]{:S(2)}, u32[]{:S(2)}) collective-permute-start(bf16[1024,256]{1,0:T(8,128)(2,1)} %pack_kv.1.kv_ref.refs_4_.refs_8_.refs_6_), channel_id=1, source_target_pairs={{0,16},{1,17},{2,50},{3,51},{4,20},{5,21},{6,54},{7,55},{8,24},{9,... | collective-permute-start | bytes 1572872 | tf_op jit(solution)/shard_map/ppermute | solution.py:51
  5.2 19.4 %collective-permute-start.3 = (bf16[1024,256]{1,0:T(8,128)(2,1)}, bf16[1024,256]{1,0:T(8,128)(2,1)S(1)}, u32[]{:S(2)}, u32[]{:S(2)}) collective-permute-start(bf16[1024,256]{1,0:T(8,128)(2,1)} %pack_kv.1.kv_ref.refs_4_.refs_8_.refs_6_), channel_id=1, source_target_pairs={{0,64},{1,193},{2,66},{3,195},{4,68},{5,197},{6,70},{7,199},{8,72}... | collective-permute-start | bytes 1572872 | tf_op jit(solution)/shard_map/ppermute | solution.py:51
  6.8 17.8 %collective-permute-start.2 = (bf16[1024,256]{1,0:T(8,128)(2,1)}, bf16[1024,256]{1,0:T(8,128)(2,1)S(1)}, u32[]{:S(2)}, u32[]{:S(2)}) collective-permute-start(bf16[1024,256]{1,0:T(8,128)(2,1)} %refs_2_.1), channel_id=1, source_target_pairs={{0,192},{1,65},{2,194},{3,67},{4,196},{5,69},{6,198},{7,71},{8,200... | collective-permute-start | bytes 1572872 | tf_op jit(solution)/shard_map/ppermute | solution.py:51
  9.1 1.0 %copy-start = (bf16[1024,256]{1,0:T(8,128)(2,1)S(1)}, bf16[1024,256]{1,0:T(8,128)(2,1)}, u32[]{:S(2)}) copy-start(bf16[1024,256]{1,0:T(8,128)(2,1)} %refs_2_.1) | copy-start | bytes 1572868
  10.1 14.5 %copy-start.1 = (bf16[1024,256]{1,0:T(8,128)(2,1)S(1)}, bf16[1024,256]{1,0:T(8,128)(2,1)}, u32[]{:S(2)}) copy-start(bf16[1024,256]{1,0:T(8,128)(2,1)} %refs_2_.1) | copy-start | bytes 1572868
  10.1 14.5 %copy-start.2 = (s32[16]{0:T(128)S(1)}, s32[16]{0:T(128)}, u32[]{:S(2)}) copy-start(s32[16]{0:T(128)} %refs_1_.9) | copy-start | bytes 196
  20.4 15.7 %collective-permute-start.1 = (bf16[1024,256]{1,0:T(8,128)(2,1)}, bf16[1024,256]{1,0:T(8,128)(2,1)S(1)}, u32[]{:S(2)}, u32[]{:S(2)}) collective-permute-start(bf16[1024,256]{1,0:T(8,128)(2,1)} %pack_kv.1.kv_ref.refs_4_.refs_8_.refs_6_), channel_id=1, source_target_pairs={{0,48},{1,49},{2,18},{3,19},{4,52},{5,53},{6,22},{7,23},{8,56},{9,... | collective-permute-start | bytes 1572872 | tf_op jit(solution)/shard_map/ppermute | solution.py:51
  23.0 15.5 %collective-permute-start.6 = (bf16[1024,256]{1,0:T(8,128)(2,1)S(1)}, bf16[1024,256]{1,0:T(8,128)(2,1)S(1)}, u32[]{:S(2)}, u32[]{:S(2)}) collective-permute-start(bf16[1024,256]{1,0:T(8,128)(2,1)S(1)} %collective-permute-done.refs_6_.refs_9_.refs_7_), channel_id=1, source_target_pairs={{0,64},{1,193},{2,66},{3,195},{4,68},{5,197},{6,70},{7,199},{8,72}... | collective-permute-start | bytes 1572872 | tf_op jit(solution)/shard_map/ppermute | solution.py:51
  36.1 12.8 %collective-permute-start.5 = (bf16[1024,256]{1,0:T(8,128)(2,1)S(1)}, bf16[1024,256]{1,0:T(8,128)(2,1)S(1)}, u32[]{:S(2)}, u32[]{:S(2)}) collective-permute-start(bf16[1024,256]{1,0:T(8,128)(2,1)S(1)} %collective-permute-done.refs_6_.refs_9_.refs_7_), channel_id=1, source_target_pairs={{0,16},{1,17},{2,50},{3,51},{4,20},{5,21},{6,54},{7,55},{8,24},{9,... | collective-permute-start | bytes 1572872 | tf_op jit(solution)/shard_map/ppermute | solution.py:51
  36.9 15.1 %collective-permute-start.4 = (bf16[1024,256]{1,0:T(8,128)(2,1)S(1)}, bf16[1024,256]{1,0:T(8,128)(2,1)S(1)}, u32[]{:S(2)}, u32[]{:S(2)}) collective-permute-start(bf16[1024,256]{1,0:T(8,128)(2,1)S(1)} %collective-permute-done.1.refs_5_.refs_10_.refs_8_), channel_id=1, source_target_pairs={{0,64},{1,193},{2,66},{3,195},{4,68},{5,197},{6,70},{7,199},{8,72}... | collective-permute-start | bytes 1572872 | tf_op jit(solution)/shard_map/ppermute | solution.py:51
  48.9 10.3 %collective-permute-start.7 = (bf16[1024,256]{1,0:T(8,128)(2,1)S(1)}, bf16[1024,256]{1,0:T(8,128)(2,1)S(1)}, u32[]{:S(2)}, u32[]{:S(2)}) collective-permute-start(bf16[1024,256]{1,0:T(8,128)(2,1)S(1)} %collective-permute-done.5.refs_4_.refs_11_.refs_9_), channel_id=1, source_target_pairs={{0,64},{1,193},{2,66},{3,195},{4,68},{5,197},{6,70},{7,199},{8,72}... | collective-permute-start | bytes 1572872 | tf_op jit(solution)/shard_map/ppermute | solution.py:51
  62.2 10.8 %collective-permute-start.8 = (bf16[272,1024]{1,0:T(8,128)(2,1)S(1)}, bf16[272,1024]{1,0:T(8,128)(2,1)S(1)}, u32[]{:S(2)}, u32[]{:S(2)}) collective-permute-start(bf16[272,1024]{1,0:T(8,128)(2,1)S(1)} %away.1), channel_id=1, source_target_pairs={{0,192},{1,65},{2,194},{3,67},{4,196},{5,69},{6,198},{7,71},{8,200... | collective-permute-start | bytes 1671176 | tf_op jit(solution)/shard_map/ppermute | solution.py:51

commit v5 on v4

--- a/solution.py
+++ b/solution.py
@@ -61,13 +61,13 @@
         vt[:HD, tile] = kv_ref[tile, HD:]
 
 
-def absorb(kb, vt, q_ref, acc, shift):
-    scores = [dot_last(kb[...], head(q_ref, 0)), None]
-    for h in range(QH):
-        if h + 1 < QH:
-            scores[h + 1] = dot_last(kb[...], head(q_ref, h + 1))
-        weights = jnp.exp2(scores[h] * SCALE - shift[h]).astype(BF16)
+def absorb(kb, vt, q_ref, acc, shift, heads):
+    scores = dot_last(kb[...], head(q_ref, heads[0]))
+    for n, h in enumerate(heads):
+        upcoming = dot_last(kb[...], head(q_ref, heads[n + 1])) if n + 1 < len(heads) else None
+        weights = jnp.exp2(scores * SCALE - shift[h]).astype(BF16)
         acc[h] += dot_mid(vt[...], weights)
+        scores = upcoming
 
 
 OWN, NEAR_A, NEAR_B, FAR = range(4)
@@ -113,7 +113,7 @@
 SCRATCH = [pltpu.VMEM((TOK, HD), BF16), pltpu.VMEM((ROWS, TOK), BF16), pltpu.SMEM((16,), jnp.int32)]
 
 
-def run_units(meta, order, q_refs, q_ids, kv_refs, blocks, accs, shifts, kb, vt, flags):
+def run_units(meta, order, q_refs, q_ids, kv_refs, blocks, accs, shifts, kb, vt, flags, heads=(0, 1)):
     nq, nb = len(q_ids), len(blocks)
     vt[HD:, :] = jnp.ones((8, TOK), BF16)
     for n, block in enumerate(blocks):
@@ -137,7 +137,7 @@
             def query(q):
                 @pl.when(flags[n * nq + q] > 0)
                 def _():
-                    absorb(kb, vt, q_refs.at[q], accs.at[q], shifts.at[q])
+                    absorb(kb, vt, q_refs.at[q], accs.at[q], shifts.at[q], heads)
 
             if nq == 1:
                 query(0)
@@ -218,7 +218,7 @@
                 shift[0, h, :, cols] = new
 
 
-def closing(meta, order, q, q_id, kvs, blocks, state, everything, pack):
+def closing(meta, order, q, q_id, kvs, blocks, state, everything, pack, heads=(0, 1)):
     nk, ne = len(kvs), len(everything)
     place = 0 if q_id == 2 else 1
 
@@ -233,17 +233,18 @@
         else:
             acc, shift, buf, q_one, kb, vt, flags = rest
         at = place if old_acc.shape[0] == 2 else 0
-        acc[0] = old_acc[at]
+        for h in heads:
+            acc[0, h] = old_acc[at, h]
         shift[0] = old_shift[at]
         q_one[0] = q_ref[...]
-        run_units(meta_ref, order_ref, q_one, [q_id], kv_refs, blocks, acc, shift, kb, vt, flags)
+        run_units(meta_ref, order_ref, q_one, [q_id], kv_refs, blocks, acc, shift, kb, vt, flags, heads)
         if not ne:
             return
         query_rank = order_ref[meta_ref[q_id]]
         active = jnp.int32(0)
         for n in range(8):
             active += (rank_of(meta_ref, order_ref, n // 4, n % 4) <= query_rank).astype(jnp.int32)
-        totals = jnp.concatenate([acc[0, h, HD:HD + 1, :] for h in range(QH)], axis=0)
+        totals = jnp.concatenate([acc[0, h, HD:HD + 1, :] for h in heads], axis=0)
         fine = jnp.logical_and(totals > 2.0 ** -60, totals < 2.0 ** 100)
         faults = jnp.sum(jnp.where(fine, 0.0, 1.0))
 
@@ -252,23 +253,23 @@
             recompute(meta_ref, order_ref, q_id, q_ref, all_refs, acc, shift, buf, kb, vt)
 
         if pack:
-            for h in range(QH):
+            for n, h in enumerate(heads):
                 total = acc[0, h, HD:HD + 1, :]
                 empty = total <= 0.0
                 safe = jnp.where(empty, 1.0, total)
-                sent[h * HD:(h + 1) * HD, :] = (acc[0, h, :HD, :] * (1.0 / safe)).astype(BF16)
+                sent[n * HD:(n + 1) * HD, :] = (acc[0, h, :HD, :] * (1.0 / safe)).astype(BF16)
                 level = jnp.where(empty, -1e30, shift[0, h] + jnp.log2(safe))
                 first = level.astype(BF16).astype(F32)
                 second = (level - first).astype(BF16).astype(F32)
                 third = level - first - second
-                row = lax.broadcasted_iota(jnp.int32, (8, TOK), 0)
+                row = lax.broadcasted_iota(jnp.int32, (16, TOK), 0)
                 packed = jnp.where(row == 0, first, jnp.where(row == 1, second, third))
-                sent[QH * HD + 8 * h:QH * HD + 8 * h + 8, :] = packed.astype(BF16)
+                sent[len(heads) * HD + 16 * n:len(heads) * HD + 16 * n + 16, :] = packed.astype(BF16)
 
     state_shapes = [((1,) + ACC, F32), ((1,) + SHIFT, F32)]
     scratch = [pltpu.VMEM((TOK, 2 * HD), BF16), pltpu.VMEM((1, TOK, QH * HD), BF16)] + SCRATCH
     if pack:
-        out_shape = jax.ShapeDtypeStruct((QH * HD + 16, TOK), BF16)
+        out_shape = jax.ShapeDtypeStruct((len(heads) * (HD + 16), TOK), BF16)
         out_specs = VMEM
         scratch = [pltpu.VMEM(*s) for s in state_shapes] + scratch
     else:
@@ -288,17 +289,16 @@
     )(meta, order, q, *kvs, *state, *everything)
 
 
-def join_kernel(acc, shift, came, out):
-    for h in range(QH):
+def join_kernel(acc, shift, came_0, came_1, out):
+    for h, came in enumerate((came_0, came_1)):
         total = acc[0, h, HD:HD + 1, :]
         here = shift[0, h] + jnp.log2(total)
-        at = QH * HD + 8 * h
-        level = came[at:at + 8, :].astype(F32)
+        level = came[HD:HD + 16, :].astype(F32)
         there = level[0:1] + level[1:2] + level[2:3]
         top = jnp.maximum(here, there)
         own, far = jnp.exp2(here - top), jnp.exp2(there - top)
         both = own + far
-        mixed = acc[0, h, :HD, :] * (own / (total * both)) + came[h * HD:(h + 1) * HD, :].astype(F32) * (far / both)
+        mixed = acc[0, h, :HD, :] * (own / (total * both)) + came[:HD, :].astype(F32) * (far / both)
         out[:, h * HD:(h + 1) * HD] = mixed.T.astype(BF16)
 
 
@@ -306,11 +306,11 @@
     return pl.pallas_call(
         join_kernel,
         out_shape=jax.ShapeDtypeStruct((TOK, QH * HD), BF16),
-        in_specs=[VMEM] * 3,
+        in_specs=[VMEM] * 4,
         out_specs=VMEM,
         compiler_params=pltpu.CompilerParams(vmem_limit_bytes=32 << 20),
         name="join",
-    )(*state, came)
+    )(*state, *came)
 
 
 def pack_kernel(keys, values, kv):
@@ -368,8 +368,10 @@
         meta, order, q1, 2, [mate_b, far], [(1, NEAR_B), (0, FAR)], state, [], False
     )
     everything = [kv, near_a, near_b, far, mate_own, mate_a, mate_b, mate_far]
-    away = closing(meta, order, q1, 2, [mate_far], [(1, FAR)], guest, everything, True)
-    came = send(away, query_perm)
+    came = []
+    for h in range(QH):
+        away = closing(meta, order, q1, 2, [mate_far], [(1, FAR)], guest, everything, True, (h,))
+        came.append(send(away, query_perm))
     own = closing(
         meta, order, q0, 0, [mate_b, far, mate_far],
         [(1, NEAR_B), (0, FAR), (1, FAR)], state, everything, False,

time: 73.2 us -> 73.7 us (level); the launches traced: 74.1 us -> 73.4 us
  Pallas kernels: 41.6 us -> 38.3 us
  starting transfers between devices: 18.8 us -> 21.5 us
    pallas_call x3 -> x4, Pallas kernels: 14.7 us -> 11.4 us  [closing(): pl.pallas_call(kernel, out_shape=out_shape, in_specs=[SMEM, SMEM] + [VMEM...]
    ppermute x9 -> x10, starting transfers between devices: 18.8 us -> 21.5 us  [send(): return lax.ppermute(array, ('ctx', 'head'), perm)]
    ppermute x9 -> x10, waiting for transfers between devices: 12.5 us -> 12.4 us  [send(): return lax.ppermute(array, ('ctx', 'head'), perm)]
  transfers between devices with their start and end apart: 9 -> 10, of which waited for: 4 -> 4; matrix products, arithmetic and copies ran while one was open for 0% -> 0% of each run, Pallas kernels for 48% -> 47%
where the time goes in v5:
time: 73.7 us; the launch traced here: 73.4 us
  Pallas kernels  38.3 us (52%)
  starting transfers between devices  21.5 us (29%)
  waiting for transfers between devices  12.4 us (17%)
  local copies, waits for them, and re-layouts  1.05 us (1%)
    ppermute x10, starting transfers between devices, send(): return lax.ppermute(array, ('ctx', 'head'), perm)  21.5 us
    pallas_call x2, Pallas kernels, stage(): pl.pallas_call(kernel, out_shape=[jax.ShapeDtypeStruct((2,) + ACC, F32),...  20.2 us
    ppermute x10, waiting for transfers between devices, send(): return lax.ppermute(array, ('ctx', 'head'), perm)  12.4 us
    pallas_call x4, Pallas kernels, closing(): pl.pallas_call(kernel, out_shape=out_shape, in_specs=[SMEM, SMEM] + [VMEM...  11.4 us
    pallas_call x1, Pallas kernels, diagonal(): pl.pallas_call(diagonal_kernel, out_shape=[jax.ShapeDtypeStruct((QH, ROWS...  3.61 us
    pallas_call x1, Pallas kernels, packed_kv(): pl.pallas_call(pack_kernel, out_shape=jax.ShapeDtypeStruct((TOK, 2 * HD),...  1.94 us
  transfers between devices with their start and end apart: 10, of which 4 were waited for; matrix products, arithmetic and copies ran while one was open for 0% of the time, Pallas kernels for 47%

profile of v5, /device:TPU:6, one launch (start us, length us, event | category | flops | bytes accessed | tf_op | source)
XLA Modules:
  0.0 73.4 jit_solution(8458821566675793273)
XLA Ops:
  0.0 1.9 %pack_kv.1.kv_ref.refs_4_.refs_8_.refs_6_ = bf16[1024,256]{1,0:T(8,128)(2,1)} custom-call(bf16[1024,128]{1,0:T(8,128)(2,1)} %keys.1, bf16[1024,128]{1,0:T(8,128)(2,1)} %values.1), custom_call_target="tpu_custom_call" | custom-call | tf_op jit(solution)/shard_map/pack_kv/pallas_call | solution.py:324
  1.9 3.3 %collective-permute-start = (bf16[1024,256]{1,0:T(8,128)(2,1)}, bf16[1024,256]{1,0:T(8,128)(2,1)S(1)}, u32[]{:S(2)}, u32[]{:S(2)}) collective-permute-start(bf16[1024,256]{1,0:T(8,128)(2,1)} %pack_kv.1.kv_ref.refs_4_.refs_8_.refs_6_), channel_id=1, source_target_pairs={{0,16},{1,17},{2,50},{3,51},{4,20},{5,21},{6,54},{7,55},{8,24},{9,... | collective-permute-start | bytes 1572872 | tf_op jit(solution)/shard_map/ppermute | solution.py:51
  5.2 1.6 %collective-permute-start.3 = (bf16[1024,256]{1,0:T(8,128)(2,1)}, bf16[1024,256]{1,0:T(8,128)(2,1)S(1)}, u32[]{:S(2)}, u32[]{:S(2)}) collective-permute-start(bf16[1024,256]{1,0:T(8,128)(2,1)} %pack_kv.1.kv_ref.refs_4_.refs_8_.refs_6_), channel_id=1, source_target_pairs={{0,64},{1,193},{2,66},{3,195},{4,68},{5,197},{6,70},{7,199},{8,72}... | collective-permute-start | bytes 1572872 | tf_op jit(solution)/shard_map/ppermute | solution.py:51
  6.8 2.2 %collective-permute-start.2 = (bf16[1024,256]{1,0:T(8,128)(2,1)}, bf16[1024,256]{1,0:T(8,128)(2,1)S(1)}, u32[]{:S(2)}, u32[]{:S(2)}) collective-permute-start(bf16[1024,256]{1,0:T(8,128)(2,1)} %refs_2_.1), channel_id=1, source_target_pairs={{0,192},{1,65},{2,194},{3,67},{4,196},{5,69},{6,198},{7,71},{8,200... | collective-permute-start | bytes 1572872 | tf_op jit(solution)/shard_map/ppermute | solution.py:51
  9.1 1.0 %copy-done = bf16[1024,256]{1,0:T(8,128)(2,1)S(1)} copy-done((bf16[1024,256]{1,0:T(8,128)(2,1)S(1)}, bf16[1024,256]{1,0:T(8,128)(2,1)}, u32[]{:S(2)}) %copy-start) | copy-done | bytes 524312
  10.1 3.6 %diagonal.1 = (f32[2,136,1024]{2,1,0:T(8,128)S(1)}, f32[2,1,1024]{2,1,0:T(1,128)S(1)}) custom-call(bf16[1024,256]{1,0:T(8,128)(2,1)S(1)} %copy-done, bf16[1024,256]{1,0:T(8,128)(2,1)} %pack_kv.1.kv_ref.refs_4_.refs_8_.refs_6_), custom_call_target="tpu_custom_call" | custom-call | flops 3221225472 | bytes 4194304 | tf_op jit(solution)/shard_map/diagonal/pallas_call | solution.py:96
  13.7 6.7 %collective-permute-done.refs_6_.refs_9_.refs_7_ = bf16[1024,256]{1,0:T(8,128)(2,1)S(1)} collective-permute-done((bf16[1024,256]{1,0:T(8,128)(2,1)}, bf16[1024,256]{1,0:T(8,128)(2,1)S(1)}, u32[]{:S(2)}, u32[]{:S(2)}) %collective-permute-start) | collective-permute-done | bytes 524320 | tf_op jit(solution)/shard_map/ppermute | solution.py:51
  20.4 2.6 %collective-permute-start.1 = (bf16[1024,256]{1,0:T(8,128)(2,1)}, bf16[1024,256]{1,0:T(8,128)(2,1)S(1)}, u32[]{:S(2)}, u32[]{:S(2)}) collective-permute-start(bf16[1024,256]{1,0:T(8,128)(2,1)} %pack_kv.1.kv_ref.refs_4_.refs_8_.refs_6_), channel_id=1, source_target_pairs={{0,48},{1,49},{2,18},{3,19},{4,52},{5,53},{6,22},{7,23},{8,56},{9,... | collective-permute-start | bytes 1572872 | tf_op jit(solution)/shard_map/ppermute | solution.py:51
  23.0 1.6 %collective-permute-start.6 = (bf16[1024,256]{1,0:T(8,128)(2,1)S(1)}, bf16[1024,256]{1,0:T(8,128)(2,1)S(1)}, u32[]{:S(2)}, u32[]{:S(2)}) collective-permute-start(bf16[1024,256]{1,0:T(8,128)(2,1)S(1)} %collective-permute-done.refs_6_.refs_9_.refs_7_), channel_id=1, source_target_pairs={{0,64},{1,193},{2,66},{3,195},{4,68},{5,197},{6,70},{7,199},{8,72}... | collective-permute-start | bytes 1572872 | tf_op jit(solution)/shard_map/ppermute | solution.py:51
  24.6 11.4 %stage.2 = (f32[2,2,136,1024]{3,2,1,0:T(8,128)S(1)}, f32[2,2,1,1024]{3,2,1,0:T(1,128)S(1)}) custom-call(s32[4]{0:T(128)S(1)} %pad_add_fusion.refs_0_, s32[16]{0:T(128)S(1)} %copy-done.2, bf16[1024,256]{1,0:T(8,128)(2,1)S(1)} %collective-permute-done.2.refs_2_, bf16[1024,256]{1,0:T(8,128)(2,1)S(1)} %copy-done.1, ...), custom_call_target="tpu_custom_call" | custom-call | flops 12884901888 | bytes 8388608 | tf_op jit(solution)/shard_map/stage/pallas_call | solution.py:177
  36.1 0.9 %collective-permute-start.5 = (bf16[1024,256]{1,0:T(8,128)(2,1)S(1)}, bf16[1024,256]{1,0:T(8,128)(2,1)S(1)}, u32[]{:S(2)}, u32[]{:S(2)}) collective-permute-start(bf16[1024,256]{1,0:T(8,128)(2,1)S(1)} %collective-permute-done.refs_6_.refs_9_.refs_7_), channel_id=1, source_target_pairs={{0,16},{1,17},{2,50},{3,51},{4,20},{5,21},{6,54},{7,55},{8,24},{9,... | collective-permute-start | bytes 1572872 | tf_op jit(solution)/shard_map/ppermute | solution.py:51
  36.9 1.6 %collective-permute-start.4 = (bf16[1024,256]{1,0:T(8,128)(2,1)S(1)}, bf16[1024,256]{1,0:T(8,128)(2,1)S(1)}, u32[]{:S(2)}, u32[]{:S(2)}) collective-permute-start(bf16[1024,256]{1,0:T(8,128)(2,1)S(1)} %collective-permute-done.1.refs_5_.refs_10_.refs_8_), channel_id=1, source_target_pairs={{0,64},{1,193},{2,66},{3,195},{4,68},{5,197},{6,70},{7,199},{8,72}... | collective-permute-start | bytes 1572872 | tf_op jit(solution)/shard_map/ppermute | solution.py:51
  38.5 8.7 %stage.3 = (f32[2,2,136,1024]{3,2,1,0:T(8,128)S(1)}, f32[2,2,1,1024]{3,2,1,0:T(1,128)S(1)}) custom-call(s32[4]{0:T(128)S(1)} %pad_add_fusion.refs_0_, s32[16]{0:T(128)S(1)} %copy-done.2, bf16[1024,256]{1,0:T(8,128)(2,1)S(1)} %collective-permute-done.2.refs_2_, bf16[1024,256]{1,0:T(8,128)(2,1)S(1)} %copy-done.1, ...), custom_call_target="tpu_custom_call" | custom-call | flops 8589934592 | bytes 8388608 | tf_op jit(solution)/shard_map/stage/pallas_call | solution.py:177
  47.3 1.6 %collective-permute-done.5.refs_4_.refs_11_.refs_9_ = bf16[1024,256]{1,0:T(8,128)(2,1)S(1)} collective-permute-done((bf16[1024,256]{1,0:T(8,128)(2,1)S(1)}, bf16[1024,256]{1,0:T(8,128)(2,1)S(1)}, u32[]{:S(2)}, u32[]{:S(2)}) %collective-permute-start.5) | collective-permute-done | bytes 524320 | tf_op jit(solution)/shard_map/ppermute | solution.py:51
  48.9 3.2 %collective-permute-start.7 = (bf16[1024,256]{1,0:T(8,128)(2,1)S(1)}, bf16[1024,256]{1,0:T(8,128)(2,1)S(1)}, u32[]{:S(2)}, u32[]{:S(2)}) collective-permute-start(bf16[1024,256]{1,0:T(8,128)(2,1)S(1)} %collective-permute-done.5.refs_4_.refs_11_.refs_9_), channel_id=1, source_target_pairs={{0,64},{1,193},{2,66},{3,195},{4,68},{5,197},{6,70},{7,199},{8,72}... | collective-permute-start | bytes 1572872 | tf_op jit(solution)/shard_map/ppermute | solution.py:51
  52.1 4.7 %guest.1 = (f32[1,2,136,1024]{3,2,1,0:T(8,128)S(1)}, f32[1,2,1,1024]{3,2,1,0:T(1,128)S(1)}) custom-call(s32[4]{0:T(128)S(1)} %pad_add_fusion.refs_0_, s32[16]{0:T(128)S(1)} %copy-done.2, bf16[1024,256]{1,0:T(8,128)(2,1)S(1)} %collective-permute-done.2.refs_2_, bf16[1024,256]{1,0:T(8,128)(2,1)S(1)} %collective-permute-done.4.refs_3_.refs_14_.refs_12_, ...), custom_call_target="tpu_custom_call" | custom-call | flops 4294967296 | bytes 8388608 | tf_op jit(solution)/shard_map/guest/pallas_call | solution.py:278
  56.8 2.5 %collective-permute-done.7.refs_5_.refs_15_.refs_3_.refs_13_ = bf16[1024,256]{1,0:T(8,128)(2,1)S(1)} collective-permute-done((bf16[1024,256]{1,0:T(8,128)(2,1)S(1)}, bf16[1024,256]{1,0:T(8,128)(2,1)S(1)}, u32[]{:S(2)}, u32[]{:S(2)}) %collective-permute-start.7) | collective-permute-done | bytes 524320 | tf_op jit(solution)/shard_map/ppermute | solution.py:51
  59.2 0.8 %away.3 = bf16[144,1024]{1,0:T(8,128)(2,1)S(1)} custom-call(s32[4]{0:T(128)S(1)} %pad_add_fusion.refs_0_, s32[16]{0:T(128)S(1)} %copy-done.2, bf16[1024,256]{1,0:T(8,128)(2,1)S(1)} %collective-permute-done.2.refs_2_, bf16[1024,256]{1,0:T(8,128)(2,1)S(1)} %collective-permute-done.7.refs_5_.refs_15_.refs_3_.refs_13_, ...), custom_call_target="tpu_custom_call" | custom-call | flops 2147483648 | bytes 8388608 | tf_op jit(solution)/shard_map/away/pallas_call | solution.py:278
  60.1 3.1 %collective-permute-start.9 = (bf16[144,1024]{1,0:T(8,128)(2,1)S(1)}, bf16[144,1024]{1,0:T(8,128)(2,1)S(1)}, u32[]{:S(2)}, u32[]{:S(2)}) collective-permute-start(bf16[144,1024]{1,0:T(8,128)(2,1)S(1)} %away.3), channel_id=1, source_target_pairs={{0,192},{1,65},{2,194},{3,67},{4,196},{5,69},{6,198},{7,71},{8,200... | collective-permute-start | bytes 884744 | tf_op jit(solution)/shard_map/ppermute | solution.py:51
  63.2 1.1 %away.2 = bf16[144,1024]{1,0:T(8,128)(2,1)S(1)} custom-call(s32[4]{0:T(128)S(1)} %pad_add_fusion.refs_0_, s32[16]{0:T(128)S(1)} %copy-done.2, bf16[1024,256]{1,0:T(8,128)(2,1)S(1)} %collective-permute-done.2.refs_2_, bf16[1024,256]{1,0:T(8,128)(2,1)S(1)} %collective-permute-done.7.refs_5_.refs_15_.refs_3_.refs_13_, ...), custom_call_target="tpu_custom_call" | custom-call | flops 2147483648 | bytes 8388608 | tf_op jit(solution)/shard_map/away/pallas_call | solution.py:278
  64.3 1.5 %collective-permute-start.8 = (bf16[144,1024]{1,0:T(8,128)(2,1)S(1)}, bf16[144,1024]{1,0:T(8,128)(2,1)S(1)}, u32[]{:S(2)}, u32[]{:S(2)}) collective-permute-start(bf16[144,1024]{1,0:T(8,128)(2,1)S(1)} %away.2), channel_id=1, source_target_pairs={{0,192},{1,65},{2,194},{3,67},{4,196},{5,69},{6,198},{7,71},{8,200... | collective-permute-start | bytes 884744 | tf_op jit(solution)/shard_map/ppermute | solution.py:51
  65.7 4.8 %home.1 = (f32[1,2,136,1024]{3,2,1,0:T(8,128)S(1)}, f32[1,2,1,1024]{3,2,1,0:T(1,128)S(1)}) custom-call(s32[4]{0:T(128)S(1)} %pad_add_fusion.refs_0_, s32[16]{0:T(128)S(1)} %copy-done.2, bf16[1024,256]{1,0:T(8,128)(2,1)S(1)} %copy-done.1, bf16[1024,256]{1,0:T(8,128)(2,1)S(1)} %collective-permute-done.4.refs_3_.refs_14_.refs_12_, ...), custom_call_target="tpu_custom_call" | custom-call | flops 6442450944 | bytes 8388608 | tf_op jit(solution)/shard_map/home/pallas_call | solution.py:278
  70.6 1.7 %collective-permute-done.8.came_0 = bf16[144,1024]{1,0:T(8,128)(2,1)S(1)} collective-permute-done((bf16[144,1024]{1,0:T(8,128)(2,1)S(1)}, bf16[144,1024]{1,0:T(8,128)(2,1)S(1)}, u32[]{:S(2)}, u32[]{:S(2)}) %collective-permute-start.8) | collective-permute-done | bytes 294944 | tf_op jit(solution)/shard_map/ppermute | solution.py:51
  72.3 1.1 %join.1 = bf16[1024,256]{1,0:T(8,128)(2,1)} custom-call(f32[1,2,136,1024]{3,2,1,0:T(8,128)S(1)} %get-tuple-element.35.acc, f32[1,2,1,1024]{3,2,1,0:T(1,128)S(1)} %get-tuple-element.36.shift, bf16[144,1024]{1,0:T(8,128)(2,1)S(1)} %collective-permute-done.8.came_0, bf16[144,1024]{1,0:T(8,128)(2,1)S(1)} %collective-permute-done.9.came_1), custom_call_target="tpu_custom_call" | custom-call | tf_op jit(solution)/shard_map/join/pallas_call | solution.py:306
  (12 shorter events, 0.1 us)
Async XLA Ops:
  1.9 18.4 %collective-permute-start = (bf16[1024,256]{1,0:T(8,128)(2,1)}, bf16[1024,256]{1,0:T(8,128)(2,1)S(1)}, u32[]{:S(2)}, u32[]{:S(2)}) collective-permute-start(bf16[1024,256]{1,0:T(8,128)(2,1)} %pack_kv.1.kv_ref.refs_4_.refs_8_.refs_6_), channel_id=1, source_target_pairs={{0,16},{1,17},{2,50},{3,51},{4,20},{5,21},{6,54},{7,55},{8,24},{9,... | collective-permute-start | bytes 1572872 | tf_op jit(solution)/shard_map/ppermute | solution.py:51
  5.2 19.4 %collective-permute-start.3 = (bf16[1024,256]{1,0:T(8,128)(2,1)}, bf16[1024,256]{1,0:T(8,128)(2,1)S(1)}, u32[]{:S(2)}, u32[]{:S(2)}) collective-permute-start(bf16[1024,256]{1,0:T(8,128)(2,1)} %pack_kv.1.kv_ref.refs_4_.refs_8_.refs_6_), channel_id=1, source_target_pairs={{0,64},{1,193},{2,66},{3,195},{4,68},{5,197},{6,70},{7,199},{8,72}... | collective-permute-start | bytes 1572872 | tf_op jit(solution)/shard_map/ppermute | solution.py:51
  6.8 17.8 %collective-permute-start.2 = (bf16[1024,256]{1,0:T(8,128)(2,1)}, bf16[1024,256]{1,0:T(8,128)(2,1)S(1)}, u32[]{:S(2)}, u32[]{:S(2)}) collective-permute-start(bf16[1024,256]{1,0:T(8,128)(2,1)} %refs_2_.1), channel_id=1, source_target_pairs={{0,192},{1,65},{2,194},{3,67},{4,196},{5,69},{6,198},{7,71},{8,200... | collective-permute-start | bytes 1572872 | tf_op jit(solution)/shard_map/ppermute | solution.py:51
  9.1 1.0 %copy-start = (bf16[1024,256]{1,0:T(8,128)(2,1)S(1)}, bf16[1024,256]{1,0:T(8,128)(2,1)}, u32[]{:S(2)}) copy-start(bf16[1024,256]{1,0:T(8,128)(2,1)} %refs_2_.1) | copy-start | bytes 1572868
  10.1 14.5 %copy-start.1 = (bf16[1024,256]{1,0:T(8,128)(2,1)S(1)}, bf16[1024,256]{1,0:T(8,128)(2,1)}, u32[]{:S(2)}) copy-start(bf16[1024,256]{1,0:T(8,128)(2,1)} %refs_2_.1) | copy-start | bytes 1572868
  10.1 14.5 %copy-start.2 = (s32[16]{0:T(128)S(1)}, s32[16]{0:T(128)}, u32[]{:S(2)}) copy-start(s32[16]{0:T(128)} %refs_1_.11) | copy-start | bytes 196
  20.4 15.7 %collective-permute-start.1 = (bf16[1024,256]{1,0:T(8,128)(2,1)}, bf16[1024,256]{1,0:T(8,128)(2,1)S(1)}, u32[]{:S(2)}, u32[]{:S(2)}) collective-permute-start(bf16[1024,256]{1,0:T(8,128)(2,1)} %pack_kv.1.kv_ref.refs_4_.refs_8_.refs_6_), channel_id=1, source_target_pairs={{0,48},{1,49},{2,18},{3,19},{4,52},{5,53},{6,22},{7,23},{8,56},{9,... | collective-permute-start | bytes 1572872 | tf_op jit(solution)/shard_map/ppermute | solution.py:51
  23.0 15.5 %collective-permute-start.6 = (bf16[1024,256]{1,0:T(8,128)(2,1)S(1)}, bf16[1024,256]{1,0:T(8,128)(2,1)S(1)}, u32[]{:S(2)}, u32[]{:S(2)}) collective-permute-start(bf16[1024,256]{1,0:T(8,128)(2,1)S(1)} %collective-permute-done.refs_6_.refs_9_.refs_7_), channel_id=1, source_target_pairs={{0,64},{1,193},{2,66},{3,195},{4,68},{5,197},{6,70},{7,199},{8,72}... | collective-permute-start | bytes 1572872 | tf_op jit(solution)/shard_map/ppermute | solution.py:51
  36.1 12.8 %collective-permute-start.5 = (bf16[1024,256]{1,0:T(8,128)(2,1)S(1)}, bf16[1024,256]{1,0:T(8,128)(2,1)S(1)}, u32[]{:S(2)}, u32[]{:S(2)}) collective-permute-start(bf16[1024,256]{1,0:T(8,128)(2,1)S(1)} %collective-permute-done.refs_6_.refs_9_.refs_7_), channel_id=1, source_target_pairs={{0,16},{1,17},{2,50},{3,51},{4,20},{5,21},{6,54},{7,55},{8,24},{9,... | collective-permute-start | bytes 1572872 | tf_op jit(solution)/shard_map/ppermute | solution.py:51
  36.9 15.1 %collective-permute-start.4 = (bf16[1024,256]{1,0:T(8,128)(2,1)S(1)}, bf16[1024,256]{1,0:T(8,128)(2,1)S(1)}, u32[]{:S(2)}, u32[]{:S(2)}) collective-permute-start(bf16[1024,256]{1,0:T(8,128)(2,1)S(1)} %collective-permute-done.1.refs_5_.refs_10_.refs_8_), channel_id=1, source_target_pairs={{0,64},{1,193},{2,66},{3,195},{4,68},{5,197},{6,70},{7,199},{8,72}... | collective-permute-start | bytes 1572872 | tf_op jit(solution)/shard_map/ppermute | solution.py:51
  48.9 10.3 %collective-permute-start.7 = (bf16[1024,256]{1,0:T(8,128)(2,1)S(1)}, bf16[1024,256]{1,0:T(8,128)(2,1)S(1)}, u32[]{:S(2)}, u32[]{:S(2)}) collective-permute-start(bf16[1024,256]{1,0:T(8,128)(2,1)S(1)} %collective-permute-done.5.refs_4_.refs_11_.refs_9_), channel_id=1, source_target_pairs={{0,64},{1,193},{2,66},{3,195},{4,68},{5,197},{6,70},{7,199},{8,72}... | collective-permute-start | bytes 1572872 | tf_op jit(solution)/shard_map/ppermute | solution.py:51
  60.1 10.5 %collective-permute-start.9 = (bf16[144,1024]{1,0:T(8,128)(2,1)S(1)}, bf16[144,1024]{1,0:T(8,128)(2,1)S(1)}, u32[]{:S(2)}, u32[]{:S(2)}) collective-permute-start(bf16[144,1024]{1,0:T(8,128)(2,1)S(1)} %away.3), channel_id=1, source_target_pairs={{0,192},{1,65},{2,194},{3,67},{4,196},{5,69},{6,198},{7,71},{8,200... | collective-permute-start | bytes 884744 | tf_op jit(solution)/shard_map/ppermute | solution.py:51
  64.3 8.0 %collective-permute-start.8 = (bf16[144,1024]{1,0:T(8,128)(2,1)S(1)}, bf16[144,1024]{1,0:T(8,128)(2,1)S(1)}, u32[]{:S(2)}, u32[]{:S(2)}) collective-permute-start(bf16[144,1024]{1,0:T(8,128)(2,1)S(1)} %away.2), channel_id=1, source_target_pairs={{0,192},{1,65},{2,194},{3,67},{4,196},{5,69},{6,198},{7,71},{8,200... | collective-permute-start | bytes 884744 | tf_op jit(solution)/shard_map/ppermute | solution.py:51
